TPU v7x, 512 devices: a whole 4x4x16 slice. The times are simulated.
512 devices in a mesh: body: 2 (over core), gx: 16 (over y, x), gy: 16 (over z).
Axes of the slice: x: 4, y: 4, z: 16, core: 2. Of those that a mesh axis runs over, the one named last changes fastest.
Arguments:
- surface_disp: float32 [2, 3, 49, 131072], P('body', None, None, ('gx', 'gy')), may hold values from -6 to 6
- proj_coords: float32 [2, 2, 36, 65536], P('body', None, None, ('gx', 'gy')), may hold values from -1 to 1
- pair_slave: int32 [2, 65536], P('body', ('gx', 'gy')), may hold values from 0 to 511
- pair_owner: int32 [2, 65536, 1], P('body', ('gx', 'gy')), may hold values from 0 to 255; in each aligned block of 256 rows (0 to 255, 256 to 511, ..., all dimensions but the last counted through in order) at most 2 rows name the same one
- send_list: int32 [2, 256, 512], P(None, ('gx', 'gy')), may hold values from 0 to 511
Outputs:
- nodal_force: float32 [2, 3, 768, 6144], P('body', None, 'gx', 'gy')
Inputs may be any that keep to these rules, and one draw needn't show every extreme that they name: `pair_owner`: within the 256 pairs of one slave tile, at most 2 name the same owner tile; in some tile exactly 2 do.
All inputs are finite; a program needn't handle non-finite values.
Results may differ from a plain program's by a relative error of at most 0.0003.
Values sent between devices are 32-bit elements; how exact they have to be, the bound alone decides.
No kernel may reach another device: no remote copies, remote signals or barrier semaphores. Data moves between devices by JAX's collectives and lax.ppermute only.
A program may use at most 64 MiB of HBM per device.

v0:
```python
import jax
import jax.numpy as jnp
from jax import lax
from jax.sharding import PartitionSpec as P

SX = 8
SY = 64


KAPPA = 2.0
SHEAR = 1.0
LOBATTO_POINTS = (
    -1.0,
    -0.830223896278567,
    -0.4688487934707142,
    0.0,
    0.4688487934707142,
    0.830223896278567,
    1.0,
)
GAUSS_POINTS = (
    -0.932469514203152,
    -0.6612093864662645,
    -0.2386191860831969,
    0.2386191860831969,
    0.6612093864662645,
    0.932469514203152,
)
GAUSS_WEIGHTS = (
    0.1713244923791704,
    0.3607615730481386,
    0.467913934572691,
    0.467913934572691,
    0.3607615730481386,
    0.1713244923791704,
)


def from_partner(value, axis, bit):
    return lax.ppermute(value, axis, [(i, i ^ 1 << bit) for i in range(lax.axis_size(axis))])


def from_behind(value, axis, by):
    length = lax.axis_size(axis)
    return lax.ppermute(value, axis, [(i, (i + by) % length) for i in range(length)])


def basis_traced(abscissa):
    points = LOBATTO_POINTS
    factors = []
    for k in range(7):
        product = jnp.ones_like(abscissa)
        for m in range(7):
            if m != k:
                product = product * ((abscissa - points[m]) * (1.0 / (points[k] - points[m])))
        factors.append(product)
    return jnp.stack(factors)


def slave_table():
    single = basis_traced(jnp.asarray(GAUSS_POINTS, jnp.float32)).T
    return (single[:, None, :, None] * single[None, :, None, :]).reshape(36, 49)


def quad_weights():
    weights = jnp.asarray(GAUSS_WEIGHTS, jnp.float32)
    return (weights[:, None] * weights[None, :]).reshape(36)


def pair_forces(slave_nodes, master_nodes, pair_coords, normal_sign):
    highest = lax.Precision.HIGHEST
    slave_basis = slave_table()
    quad_weight = quad_weights()
    first_basis = basis_traced(pair_coords[0])
    second_basis = basis_traced(pair_coords[1])
    slave_value = jnp.einsum("qi,cip->cqp", slave_basis, slave_nodes, precision=highest)
    master_grid = master_nodes.reshape(3, 7, 7, -1)
    partial_sum = jnp.einsum("lqp,cklp->ckqp", second_basis, master_grid, precision=highest)
    master_value = jnp.sum(first_basis[None] * partial_sum, axis=1)
    offset = master_value - slave_value
    normal_gap = normal_sign * offset[2]
    pressure = KAPPA * jax.nn.softplus(-normal_gap)
    traction = (
        jnp.stack([SHEAR * offset[0], SHEAR * offset[1], -normal_sign * pressure])
        * quad_weight[None, :, None]
    )
    slave_force = jnp.einsum("qi,cqp->cip", slave_basis, traction, precision=highest)
    weighted = second_basis[None] * traction[:, None]
    master_force = -jnp.einsum("kqp,clqp->cklp", first_basis, weighted, precision=highest).reshape(
        3, 49, -1
    )
    return (slave_force, master_force)


def slot_ranks(owners, tile_count):
    onehot = (owners[:, None] == jnp.arange(tile_count, dtype=jnp.int32)[None, :]).astype(jnp.int32)
    before = jnp.cumsum(onehot, axis=0) - onehot
    return jnp.sum(before * onehot, axis=1)


def cross_body(payload):
    return from_partner(payload, "body", 0)


def across_tiles(buffer):
    return lax.all_to_all(
        lax.all_to_all(buffer, "gx", split_axis=2, concat_axis=2, tiled=True),
        "gy",
        split_axis=3,
        concat_axis=3,
        tiled=True,
    )


def assemble_local(element_force, seg_x, seg_y):
    segment_grid = element_force.reshape(3, 7, 7, seg_x, seg_y)
    rim_x = from_behind(segment_grid[:, 6, :, seg_x - 1 :, :], "gx", 1)
    incoming_x = jnp.concatenate([rim_x, segment_grid[:, 6, :, : seg_x - 1, :]], axis=2)
    along_x = segment_grid[:, :6].at[:, 0].add(incoming_x)
    rim_y = from_behind(along_x[:, :, 6, :, seg_y - 1 :], "gy", 1)
    incoming_y = jnp.concatenate([rim_y, along_x[:, :, 6, :, : seg_y - 1]], axis=3)
    along_y = along_x[:, :, :6].at[:, :, 0].add(incoming_y)
    return along_y.transpose(0, 3, 1, 4, 2).reshape(3, 6 * seg_x, 6 * seg_y)


def local(surface_disp, proj_coords, pair_slave, pair_owner, send_list):
    width_x = lax.axis_size("gx")
    width_y = lax.axis_size("gy")
    tile_count = width_x * width_y
    body_side = lax.axis_index("body")
    normal_sign = 1.0 - 2.0 * body_side.astype(jnp.float32)
    own_surface = surface_disp[0]
    segment_count = own_surface.shape[-1]
    slots_total = send_list.shape[-1]
    slot_capacity = slots_total // tile_count
    own_list = jnp.where(body_side == 0, send_list[0, 0], send_list[1, 0])
    owners = pair_owner[0, :, 0]
    slot_index = owners * slot_capacity + slot_ranks(owners, tile_count)
    slave_nodes = jnp.take(own_surface, pair_slave[0], axis=2)
    outgoing = jnp.take(own_surface, own_list, axis=2)
    arrived = across_tiles(outgoing.reshape(3, 49, width_x, width_y * slot_capacity))
    received = cross_body(arrived).reshape(3, 49, slots_total)
    master_nodes = jnp.take(received, slot_index, axis=2)
    slave_force, master_force = pair_forces(slave_nodes, master_nodes, proj_coords[0], normal_sign)
    element_force = (
        jnp.zeros((3, 49, segment_count), jnp.float32).at[:, :, pair_slave[0]].add(slave_force)
    )
    slot_force = jnp.zeros((3, 49, slots_total), jnp.float32).at[:, :, slot_index].add(master_force)
    crossed = cross_body(slot_force).reshape(3, 49, width_x, width_y * slot_capacity)
    returned = across_tiles(crossed).reshape(3, 49, slots_total)
    element_force = element_force + jnp.zeros((3, 49, segment_count), jnp.float32).at[
        :, :, own_list
    ].add(returned)
    nodal = assemble_local(element_force, SX, SY)
    return nodal[None]


def solution(mesh):
    return jax.shard_map(
        local,
        mesh=mesh,
        in_specs=(
            P("body", None, None, ("gx", "gy")),
            P("body", None, None, ("gx", "gy")),
            P("body", ("gx", "gy")),
            P("body", ("gx", "gy"), None),
            P(None, ("gx", "gy"), None),
        ),
        out_specs=P("body", None, "gx", "gy"),
        check_vma=False,
    )
```

profile of v0, /device:TPU:64, one launch (start us, length us, event | category | flops | bytes accessed | tf_op | source)
XLA Modules:
  0.0 203.1 jit_solution(11280034267133910050)
XLA Ops:
  0.5 1.4 fusion.30
  1.9 1.4 copy.86
  3.3 2.6 %gather_fusion = f32[512,3,49]{2,1,0:T(4,128)} fusion(f32[3,49,512]{1,0,2:T(4,128)S(1)} %bitcast.303, s32[1024]{0:T(1024)S(1)} %pad_clamp_fusion.2), kind=kCustom, calls=%fused_computation.2 | custom fusion | bytes 604160 | tf_op jit(solution)/shard_map/jit(_take)/gather | solution.py:140
  6.0 1.3 copy.87
  7.6 1.6 reshape.1164
  9.2 7.0 %all-to-all-start = ((f32[16,1,4704]{2,1,0:T(1,128)}), f32[16,1,4704]{2,1,0:T(1,128)S(1)}, u32[]{:S(2)}, u32[]{:S(2)}) async-start(f32[16,1,4704]{2,1,0:T(1,128)} %reshape.1164), calls=%async_computation | async-start | bytes 606208 | tf_op jit(solution)/shard_map/all_to_all | solution.py:107
  17.4 7.9 %all-to-all-done = f32[16,1,4704]{2,1,0:T(1,128)S(1)} async-done(((f32[16,1,4704]{2,1,0:T(1,128)}), f32[16,1,4704]{2,1,0:T(1,128)S(1)}, u32[]{:S(2)}, u32[]{:S(2)}) %all-to-all-start) | async-done | bytes 301088 | tf_op jit(solution)/shard_map/all_to_all | solution.py:107
  25.9 1.4 reduce.9
  27.2 1.0 reshape.1165
  28.7 1.6 reshape.1166
  30.3 14.8 %all-to-all-start.1 = ((f32[16,1,4704]{2,1,0:T(1,128)}), f32[16,1,4704]{2,1,0:T(1,128)S(1)}, u32[]{:S(2)}, u32[]{:S(2)}) async-start(f32[16,1,4704]{2,1,0:T(1,128)} %reshape.1166), calls=%async_computation.1 | async-start | bytes 606208 | tf_op jit(solution)/shard_map/all_to_all | solution.py:106
  45.3 18.7 %all-to-all-done.1 = f32[16,1,4704]{2,1,0:T(1,128)S(1)} async-done(((f32[16,1,4704]{2,1,0:T(1,128)}), f32[16,1,4704]{2,1,0:T(1,128)S(1)}, u32[]{:S(2)}, u32[]{:S(2)}) %all-to-all-start.1) | async-done | bytes 301088 | tf_op jit(solution)/shard_map/all_to_all | solution.py:106
  64.0 1.4 reduce.10
  65.4 1.9 reshape.1167
  67.2 1.9 collective-permute-start
  69.2 1.4 copy.99
  70.5 1.4 copy.113
  71.9 1.3 copy.83
  73.2 1.0 gather_fusion.2
  74.4 1.4 copy.114
  75.8 1.1 select_bitcast_fusion
  77.8 1.0 gather_fusion.1
  78.8 1.1 select_bitcast_fusion.1
  79.9 1.8 reshape.1153
  81.7 8.5 %fusion = f32[3,36,256]{1,0,2:T(4,128)} fusion(f32[3,7,7,256]{2,1,0,3:T(8,128)S(1)} %reshape.1153, f32[7,36,256,1]{1,0,3,2:T(8,128)} %copy.113, f32[7,36,256]{1,0,2:T(8,128)} %copy.83), kind=kOutput, calls=%fused_computation.7 | convolution fusion | flops 16616448 | bytes 777216 | tf_op jit(solution)/shard_map/lqp,cklp->ckqp/dot_general | solution.py:78
  90.2 1.2 copy.97
  91.4 1.6 fusion.7
  93.1 1.0 copy.100
  94.1 7.4 %negate_bitcast_fusion = f32[3,7,7,256]{1,2,0,3:T(8,128)S(1)} fusion(f32[7,36,256,1]{1,0,3,2:T(8,128)} %copy.114, f32[3,36,256]{1,0,2:T(4,128)} %copy.100, f32[7,36,256]{1,0,2:T(8,128)} %copy.99), kind=kOutput, calls=%fused_computation.8 | convolution fusion | flops 16488192 | bytes 777216 | tf_op jit(solution)/shard_map/kqp,clqp->cklp/dot_general | solution.py:89
  101.5 1.2 copy.102
  103.2 8.3 %scatter_fusion.1 = f32[3,49,512]{1,0,2:T(4,128)S(1)} fusion(f32[3,49,512]{1,0,2:T(4,128)S(1)} %broadcast.1255.clone.2, s32[256]{0:T(256)S(1)} %bitcast.320, f32[256,3,49]{2,1,0:T(4,128)S(1)} %copy.103), kind=kCustom, calls=%fused_computation.4 | custom fusion | flops 37632 | bytes 452608 | tf_op jit(solution)/shard_map/scatter-add | solution.py:148
  111.8 2.6 %collective-permute-start.1 = (f32[3,49,512]{2,1,0:T(8,128)S(1)}, f32[3,49,512]{2,1,0:T(8,128)S(1)}, u32[]{:S(2)}, u32[]{:S(2)}) collective-permute-start(f32[3,49,512]{2,1,0:T(8,128)S(1)} %copy.104), channel_id=1, source_target_pairs={{0,256},{256,0},{1,257},{257,1},{2,258},{258,2},{3,259},{259,3},{4... | collective-permute-start | bytes 903176 | tf_op jit(solution)/shard_map/ppermute | solution.py:40
  114.5 1.0 collective-permute-done.1
  116.8 12.5 %all_to_all.20 = f32[16,1,4704]{2,1,0:T(1,128)S(1)} all-to-all(f32[16,1,4704]{2,1,0:T(1,128)S(1)} %reshape.1168), channel_id=1, replica_groups=mesh['body'=2,'gx'=16,'gy'=16] {'gx'}, dimensions={0} | all-to-all | bytes 602112 | tf_op jit(solution)/shard_map/all_to_all | solution.py:107
  129.3 1.4 reduce.11
  130.7 1.0 reshape.1169
  132.1 1.6 reshape.1170
  133.8 5.9 %all-to-all-start.3 = ((f32[16,1,4704]{2,1,0:T(1,128)}), f32[16,1,4704]{2,1,0:T(1,128)S(1)}, u32[]{:S(2)}, u32[]{:S(2)}) async-start(f32[16,1,4704]{2,1,0:T(1,128)} %reshape.1170), calls=%async_computation.3 | async-start | bytes 606208 | tf_op jit(solution)/shard_map/all_to_all | solution.py:106
  140.4 8.3 %scatter_fusion = f32[3,49,512]{1,0,2:T(4,128)S(1)} fusion(f32[3,49,512]{1,0,2:T(4,128)S(1)} %broadcast.1255.clone, s32[256]{0:T(256)S(1)} %bitcast.323, f32[256,3,49]{2,1,0:T(4,128)S(1)} %copy.98), kind=kCustom, calls=%fused_computation.3 | custom fusion | flops 37632 | bytes 452608 | tf_op jit(solution)/shard_map/scatter-add | solution.py:146
  148.7 10.4 %all-to-all-done.3 = f32[16,1,4704]{2,1,0:T(1,128)S(1)} async-done(((f32[16,1,4704]{2,1,0:T(1,128)}), f32[16,1,4704]{2,1,0:T(1,128)S(1)}, u32[]{:S(2)}, u32[]{:S(2)}) %all-to-all-start.3) | async-done | bytes 301088 | tf_op jit(solution)/shard_map/all_to_all | solution.py:106
  159.1 1.4 reduce.12
  162.4 16.7 %scatter_fusion.2 = f32[3,49,512]{1,0,2:T(4,128)S(1)} fusion(f32[3,49,512]{1,0,2:T(4,128)S(1)} %broadcast.1255.clone.1, s32[512]{0:T(512)S(1)} %bitcast.315, f32[512,3,49]{2,1,0:T(4,128)S(1)} %copy.109), kind=kCustom, calls=%fused_computation.5 | custom fusion | flops 75264 | bytes 905216 | tf_op jit(solution)/shard_map/scatter-add | solution.py:153
  179.9 2.4 %collective-permute-start.2 = (f32[3,7,1,64]{3,2,1,0:T(1,128)S(1)}, f32[3,7,1,64]{3,2,1,0:T(1,128)S(1)}, u32[]{:S(2)}, u32[]{:S(2)}) collective-permute-start(f32[3,7,1,64]{3,2,1,0:T(1,128)S(1)} %slice_bitcast_fusion.3), channel_id=1, source_target_pairs={{0,16},{16,32},{32,48},{48,64},{64,80},{80,96},{96,112},{112,128},... | collective-permute-start | bytes 16136 | tf_op jit(solution)/shard_map/ppermute | solution.py:45
  182.3 6.4 %collective-permute-done.2 = f32[3,7,1,64]{3,2,1,0:T(1,128)S(1)} collective-permute-done((f32[3,7,1,64]{3,2,1,0:T(1,128)S(1)}, f32[3,7,1,64]{3,2,1,0:T(1,128)S(1)}, u32[]{:S(2)}, u32[]{:S(2)}) %collective-permute-start.2) | collective-permute-done | bytes 5408 | tf_op jit(solution)/shard_map/ppermute | solution.py:45
  188.9 2.7 %collective-permute-start.3 = (f32[3,6,8,1]{3,2,1,0:T(8,128)S(1)}, f32[3,6,8,1]{3,2,1,0:T(8,128)S(1)}, u32[]{:S(2)}, u32[]{:S(2)}) collective-permute-start(f32[3,6,8,1]{3,2,1,0:T(8,128)S(1)} %slice_bitcast_fusion.2), channel_id=1, source_target_pairs={{0,1},{1,2},{2,3},{3,4},{4,5},{5,6},{6,7},{7,8},{8,9},{9,10},{10,1... | collective-permute-start | bytes 1736 | tf_op jit(solution)/shard_map/ppermute | solution.py:45
  191.6 3.5 %collective-permute-done.3 = f32[3,6,8,1]{3,2,1,0:T(8,128)S(1)} collective-permute-done((f32[3,6,8,1]{3,2,1,0:T(8,128)S(1)}, f32[3,6,8,1]{3,2,1,0:T(8,128)S(1)}, u32[]{:S(2)}, u32[]{:S(2)}) %collective-permute-start.3) | collective-permute-done | bytes 608 | tf_op jit(solution)/shard_map/ppermute | solution.py:45
  195.2 3.0 %copy.112 = f32[3,8,6,64,6]{4,3,2,1,0:T(8,128)} copy(f32[3,8,6,64,6]{3,1,4,2,0:T(8,128)S(1)} %bitcast.306) | data formatting | bytes 442368 | tf_op jit(solution)/shard_map/transpose | solution.py:123
  198.2 4.9 %broadcast_in_dim_reshape.4 = f32[1,3,48,384]{3,2,1,0:T(8,128)} reshape(f32[3,8,6,64,6]{4,3,2,1,0:T(8,128)} %copy.112) | data formatting | bytes 442368 | tf_op jit(solution)/shard_map/broadcast_in_dim;reshape | solution.py:155
  (83 shorter events, 10.2 us)
Async XLA Ops:
  3.3 12.9 %copy-start = (f32[1,2,36,256]{3,1,2,0:T(2,128)S(1)}, f32[1,2,36,256]{3,1,2,0:T(2,128)}, u32[]{:S(2)}) copy-start(f32[1,2,36,256]{3,1,2,0:T(2,128)} %param.14) | copy-start | bytes 221188
  6.0 10.7 %copy-start.1 = (s32[1,256,1]{1,2,0:T(1,128)S(1)}, s32[1,256,1]{1,2,0:T(1,128)}, u32[]{:S(2)}) copy-start(s32[1,256,1]{1,2,0:T(1,128)} %param.16) | copy-start | bytes 3076
  7.3 10.0 %copy-start.4 = (f32[6]{0:T(128)S(1)}, f32[6]{0:T(128)}, u32[]{:S(2)}) copy-start(f32[6]{0:T(128)} %constant.210.clone) | copy-start | bytes 76
  7.3 10.1 %copy-start.3 = (s32[1,256]{1,0:T(1,128)S(1)}, s32[1,256]{1,0:T(1,128)}, u32[]{:S(2)}) copy-start(s32[1,256]{1,0:T(1,128)} %param.15) | copy-start | bytes 3076
  9.2 16.2 %all-to-all-start = ((f32[16,1,4704]{2,1,0:T(1,128)}), f32[16,1,4704]{2,1,0:T(1,128)S(1)}, u32[]{:S(2)}, u32[]{:S(2)}) async-start(f32[16,1,4704]{2,1,0:T(1,128)} %reshape.1164), calls=%async_computation | async-start | bytes 606208 | tf_op jit(solution)/shard_map/all_to_all | solution.py:107
  17.0 28.1 %copy-start.2 = (f32[6,7]{1,0:T(8,128)S(1)}, f32[6,7]{1,0:T(8,128)}, u32[]{:S(2)}) copy-start(f32[6,7]{1,0:T(8,128)} %constant.305) | copy-start | bytes 508
  30.3 33.7 %all-to-all-start.1 = ((f32[16,1,4704]{2,1,0:T(1,128)}), f32[16,1,4704]{2,1,0:T(1,128)S(1)}, u32[]{:S(2)}, u32[]{:S(2)}) async-start(f32[16,1,4704]{2,1,0:T(1,128)} %reshape.1166), calls=%async_computation.1 | async-start | bytes 606208 | tf_op jit(solution)/shard_map/all_to_all | solution.py:106
  67.2 9.7 %collective-permute-start = (f32[3,49,16,32]{1,2,0,3:T(8,128)}, f32[3,49,16,32]{1,2,0,3:T(8,128)S(1)}, u32[]{:S(2)}, u32[]{:S(2)}) collective-permute-start(f32[3,49,16,32]{1,2,0,3:T(8,128)} %bitcast.311), channel_id=1, source_target_pairs={{0,256},{256,0},{1,257},{257,1},{2,258},{258,2},{3,259},{259,3},{4... | collective-permute-start | bytes 903176 | tf_op jit(solution)/shard_map/ppermute | solution.py:40
  111.8 3.7 %collective-permute-start.1 = (f32[3,49,512]{2,1,0:T(8,128)S(1)}, f32[3,49,512]{2,1,0:T(8,128)S(1)}, u32[]{:S(2)}, u32[]{:S(2)}) collective-permute-start(f32[3,49,512]{2,1,0:T(8,128)S(1)} %copy.104), channel_id=1, source_target_pairs={{0,256},{256,0},{1,257},{257,1},{2,258},{258,2},{3,259},{259,3},{4... | collective-permute-start | bytes 903176 | tf_op jit(solution)/shard_map/ppermute | solution.py:40
  133.8 25.4 %all-to-all-start.3 = ((f32[16,1,4704]{2,1,0:T(1,128)}), f32[16,1,4704]{2,1,0:T(1,128)S(1)}, u32[]{:S(2)}, u32[]{:S(2)}) async-start(f32[16,1,4704]{2,1,0:T(1,128)} %reshape.1170), calls=%async_computation.3 | async-start | bytes 606208 | tf_op jit(solution)/shard_map/all_to_all | solution.py:106
  179.9 8.9 %collective-permute-start.2 = (f32[3,7,1,64]{3,2,1,0:T(1,128)S(1)}, f32[3,7,1,64]{3,2,1,0:T(1,128)S(1)}, u32[]{:S(2)}, u32[]{:S(2)}) collective-permute-start(f32[3,7,1,64]{3,2,1,0:T(1,128)S(1)} %slice_bitcast_fusion.3), channel_id=1, source_target_pairs={{0,16},{16,32},{32,48},{48,64},{64,80},{80,96},{96,112},{112,128},... | collective-permute-start | bytes 16136 | tf_op jit(solution)/shard_map/ppermute | solution.py:45
  188.9 6.2 %collective-permute-start.3 = (f32[3,6,8,1]{3,2,1,0:T(8,128)S(1)}, f32[3,6,8,1]{3,2,1,0:T(8,128)S(1)}, u32[]{:S(2)}, u32[]{:S(2)}) collective-permute-start(f32[3,6,8,1]{3,2,1,0:T(8,128)S(1)} %slice_bitcast_fusion.2), channel_id=1, source_target_pairs={{0,1},{1,2},{2,3},{3,4},{4,5},{5,6},{6,7},{7,8},{8,9},{9,10},{10,1... | collective-permute-start | bytes 1736 | tf_op jit(solution)/shard_map/ppermute | solution.py:45
where the time goes:
time: 204 us; the launch traced here: 203 us
  waiting for transfers between devices  48 us (24%)
  other arithmetic  44.1 us (22%)
  local copies, waits for them, and re-layouts  42.7 us (21%)
  starting transfers between devices  37.3 us (18%)
  matrix products  17.8 us (9%)
  blocking collectives  12.5 us (6%)
    all_to_all x2, waiting for transfers between devices, across_tiles(): lax.all_to_all(lax.all_to_all(buffer, 'gx', split_axis=2, concat_axis=2,...  29.1 us
    all_to_all x2, starting transfers between devices, across_tiles(): lax.all_to_all(lax.all_to_all(buffer, 'gx', split_axis=2, concat_axis=2,...  20.6 us
    scatter-add x1, other arithmetic, local(): element_force = element_force + jnp.zeros((3, 49, segment_count), jnp.flo...  16.7 us
    all_to_all x1, blocking collectives, across_tiles(): lax.all_to_all(buffer, 'gx', split_axis=2, concat_axis=2, tiled=True)  12.5 us
    unnamed x20, local copies, waits for them, and re-layouts  12 us
    ppermute x2, waiting for transfers between devices, from_behind(): lax.ppermute(value, axis, [(i, (i + by) % length) for i in range(length)])  9.89 us
    dot_general x1, matrix products, pair_forces(): jnp.einsum('lqp,cklp->ckqp', second_basis, master_grid, precision=highest)  8.46 us
    scatter-add x1, other arithmetic, local(): jnp.zeros((3, 49, segment_count), jnp.float32).at[:, :, pair_slave[0]]  8.33 us
  transfers between devices with their start and end apart: 7, of which 6 were waited for; matrix products, arithmetic and copies ran while one was open for 9% of the time, Pallas kernels for 0%

commit v1 on v0

v1 whole, which is shorter than its diff:
```python
import jax
import jax.numpy as jnp
import numpy as np
from jax import lax
from jax.experimental import pallas as pl
from jax.experimental.pallas import tpu as pltpu
from jax.sharding import PartitionSpec as P

SX = 8
SY = 64
TILES = 256
KAPPA = 2.0
SHEAR = 1.0
LOBATTO_POINTS = (
    -1.0,
    -0.830223896278567,
    -0.4688487934707142,
    0.0,
    0.4688487934707142,
    0.830223896278567,
    1.0,
)
GAUSS_POINTS = (
    -0.932469514203152,
    -0.6612093864662645,
    -0.2386191860831969,
    0.2386191860831969,
    0.6612093864662645,
    0.932469514203152,
)
GAUSS_WEIGHTS = (
    0.1713244923791704,
    0.3607615730481386,
    0.467913934572691,
    0.467913934572691,
    0.3607615730481386,
    0.1713244923791704,
)
F32 = jnp.float32
BF16 = jnp.bfloat16
HIGHEST = lax.Precision.HIGHEST
NN = (((1,), (0,)), ((), ()))
NT = (((1,), (1,)), ((), ()))


def lagrange_scales():
    scales = []
    for k in range(7):
        product = 1.0
        for m in range(7):
            if m != k:
                product /= LOBATTO_POINTS[k] - LOBATTO_POINTS[m]
        scales.append(product)
    return scales


def tables():
    points = np.array(LOBATTO_POINTS)
    gauss = np.array(GAUSS_POINTS)
    single = np.ones((6, 7))
    for k in range(7):
        for m in range(7):
            if m != k:
                single[:, k] *= (gauss - points[m]) / (points[k] - points[m])
    basis = np.einsum("ak,bm->abkm", single, single).reshape(36, 49)
    to_points = np.zeros((120, 192), np.float32)
    to_nodes = np.zeros((192, 120), np.float32)
    for c in range(3):
        to_points[40 * c : 40 * c + 36, 49 * c : 49 * c + 49] = basis
    for row in range(192):
        c, k, m = node_of_row(row)
        to_nodes[row, 40 * c : 40 * c + 36] = basis[:, 7 * k + m]
    spread = np.zeros((512, 384), np.float32)
    for g in range(8):
        for lc in range(64):
            y = 6 * lc + g if g < 7 else (0 if lc == 63 else -1)
            if 0 <= y < 384:
                spread[64 * g + lc, y] = 1.0
    stack = np.zeros((144, 216), np.float32)
    for la in range(9):
        for j in range(24):
            if la < 8 and j < 21:
                c, x = j // 7, 6 * la + j % 7
            elif la == 8 and j >= 21:
                c, x = j - 21, 0
            else:
                continue
            if x < 48:
                stack[48 * c + x, 24 * la + j] = 1.0
    return (
        jnp.asarray(to_points),
        jnp.asarray(to_nodes),
        jnp.asarray(spread, BF16),
        jnp.asarray(stack, BF16),
    )


def node_of_row(row):
    g, j = divmod(row, 24)
    m = min(g, 6)
    if j < 21:
        return j // 7, j % 7, m
    return j - 21, 6, m


def rows_of_node(c, k, m):
    rows = [24 * m + 7 * c + k]
    if k == 6:
        rows.append(24 * m + 21 + c)
    if m == 6:
        rows.append(168 + 7 * c + k)
    if k == 6 and m == 6:
        rows.append(189 + c)
    return rows


def split(value):
    high = value.astype(BF16)
    return high, (value - high.astype(F32)).astype(BF16)


def dot(a, b, dims):
    return lax.dot_general(a, b, dims, preferred_element_type=F32)


def onehot(condition):
    return jnp.where(condition, 1.0, 0.0).astype(BF16)


def iota(shape, dim):
    return lax.broadcasted_iota(jnp.int32, shape, dim)


def load_surface(surf_ref, scratch):
    scratch[144:, :] = jnp.zeros((scratch.shape[0] - 144, 512), F32)
    for j in range(4):
        scratch[0:147, 128 * j : 128 * j + 128] = surf_ref[pl.ds(j, 147, stride=4), :]


def gather_kernel(body_ref, list_ref, surf_ref, out_ref, surf_scr, rows_scr):
    mine = jnp.where(body_ref[0] == 0, list_ref[0], list_ref[1])
    column = jnp.transpose(jnp.broadcast_to(mine.astype(F32), (8, 512)))[:, 0:1]
    pick = onehot(column.astype(jnp.int32) == iota((512, 512), 1))
    load_surface(surf_ref, surf_scr)
    high, low = split(surf_scr[...])
    rows = dot(pick, high, NT) + dot(pick, low, NT)
    rows_scr[0] = rows[:, :128]
    rows_scr[1] = rows[:, 128:]
    left = iota((256, 128), 1) < 64
    out_ref[:, 0:128] = rows_scr[0, pl.ds(0, 256, stride=2), :]
    out_ref[:, 128:256] = rows_scr[0, pl.ds(1, 256, stride=2), :]
    out_ref[:, 256:384] = jnp.where(
        left,
        rows_scr[1, pl.ds(0, 256, stride=2), :],
        pltpu.roll(rows_scr[1, pl.ds(1, 256, stride=2), :], 64, 1),
    )


def slave_kernel(surf_ref, slave_ref, coord_ref, owner_ref, table_ref, out_ref, surf_scr):
    load_surface(surf_ref, surf_scr)
    at_points = lax.dot_general(
        table_ref[...], surf_scr[...], NN, precision=HIGHEST, preferred_element_type=F32
    )
    pick = onehot(iota((512, 256), 0) == slave_ref[...])
    high, low = split(at_points)
    out_ref[0:120, :] = dot(high, pick, NN) + dot(low, pick, NN)
    out_ref[120:200, :] = jnp.zeros((80, 256), F32)
    for e in range(2):
        for j in range(2):
            out_ref[120 + 40 * e : 156 + 40 * e, 128 * j : 128 * j + 128] = coord_ref[
                pl.ds(2 * j + e, 36, stride=4), :
            ]
    out_ref[200:208, :] = jnp.broadcast_to(owner_ref[...].astype(F32), (8, 256))


def unpack(buffer):
    turned = [jnp.transpose(buffer[:, 128 * i : 128 * i + 128]) for i in range(3)]
    return (
        jnp.concatenate([turned[0], turned[2][:64]], axis=0),
        jnp.concatenate([turned[1], turned[2][64:]], axis=0),
    )


def pair_kernel(
    sign_ref, buffer_ref, pack_ref, out_ref, traction_ref, master_scr, basis_scr, force_scr
):
    sign = sign_ref[0]
    owner = pack_ref[200:201, :].astype(jnp.int32)
    named = owner == iota((256, 256), 0)
    pick = onehot(named)
    earlier = onehot(iota((256, 256), 0) < iota((256, 256), 1))
    before = dot(pick, earlier, NN)
    picks = [onehot(named & (before < 0.5)), onehot(named & (before > 0.5))]
    master = jnp.zeros((192, 256), F32)
    for half, chosen in zip(unpack(buffer_ref[...]), picks):
        high, low = split(half)
        master = master + dot(high, chosen, NN) + dot(low, chosen, NN)
    master_scr[...] = master
    scales = lagrange_scales()
    for e in range(2):
        coord = pack_ref[120 + 40 * e : 160 + 40 * e, :]
        parts = [coord - point for point in LOBATTO_POINTS]
        prefix = [None, parts[0]]
        for i in range(1, 6):
            prefix.append(prefix[-1] * parts[i])
        suffix = [None] * 7
        suffix[5] = parts[6]
        for i in range(4, -1, -1):
            suffix[i] = suffix[i + 1] * parts[i + 1]
        for k in range(7):
            if k == 0:
                value = suffix[0]
            elif k == 6:
                value = prefix[6]
            else:
                value = prefix[k] * suffix[k]
            basis_scr[e, k] = value * scales[k]
    point = iota((8, 128), 0)
    for t in range(5):
        q = point + 8 * t
        a = jnp.zeros((8, 128), jnp.int32)
        for i in range(1, 6):
            a = a + jnp.where(q >= 6 * i, 1, 0)
        b = q - 6 * a
        weight = jnp.ones((8, 128), F32)
        for index in (a, b):
            near = jnp.where(index > 2, 5 - index, index)
            weight = weight * jnp.where(
                near == 0,
                GAUSS_WEIGHTS[0],
                jnp.where(near == 1, GAUSS_WEIGHTS[1], GAUSS_WEIGHTS[2]),
            )
        weight = jnp.where(q < 36, weight, 0.0)
        rows = slice(8 * t, 8 * t + 8)
        for j in range(2):
            lanes = slice(128 * j, 128 * j + 128)
            first = [basis_scr[0, k, rows, lanes] for k in range(7)]
            second = [basis_scr[1, k, rows, lanes] for k in range(7)]
            for c in range(3):
                total = None
                for k in range(7):
                    inner = None
                    for m in range(7):
                        i = 49 * c + 7 * k + m
                        term = second[m] * master_scr[i : i + 1, lanes]
                        inner = term if inner is None else inner + term
                    inner = first[k] * inner
                    total = inner if total is None else total + inner
                offset = total - pack_ref[40 * c + 8 * t : 40 * c + 8 * t + 8, lanes]
                if c < 2:
                    traction = SHEAR * offset
                else:
                    v = -(sign * offset)
                    pressure = jnp.maximum(v, 0.0) + jnp.log1p(jnp.exp(-jnp.abs(v)))
                    traction = -sign * (KAPPA * pressure)
                traction_ref[40 * c + 8 * t : 40 * c + 8 * t + 8, lanes] = weight * traction
    force_scr[192:256, :] = jnp.zeros((64, 256), F32)
    for j in range(2):
        lanes = slice(128 * j, 128 * j + 128)
        for k in range(7):
            first = basis_scr[0, k, :, lanes]
            weighted = [-first * traction_ref[40 * c : 40 * c + 40, lanes] for c in range(3)]
            for m in range(7):
                second = basis_scr[1, m, :, lanes]
                for c in range(3):
                    row = jnp.sum(weighted[c] * second, axis=0, keepdims=True)
                    for at in rows_of_node(c, k, m):
                        force_scr[at : at + 1, lanes] = row
    high, low = split(force_scr[...])
    to_owner = [dot(chosen, high, NT) + dot(chosen, low, NT) for chosen in picks]
    lane = iota((256, 128), 1)
    row = iota((256, 128), 0)
    wrap = (row & 15) == 0

    def shift_x(value):
        return jnp.concatenate([value[240:], value[:240]], axis=0)

    def shift_y(value):
        return jnp.where(wrap, pltpu.roll(value, 241, 0), pltpu.roll(value, 1, 0))

    rim = jnp.zeros((256, 128), jnp.bool_)
    for g in range(6):
        rim = rim | ((lane >= 24 * g + 21) & (lane < 24 * g + 24))
    tails = []
    for r in range(2):
        head = to_owner[r][:, :128]
        out_ref[:, 128 * r : 128 * r + 128] = jnp.where(rim, shift_x(head), head)
        tail = to_owner[r][:, 128:]
        tail = jnp.where(lane >= 40, shift_y(tail), tail)
        edge = ((lane >= 13) & (lane < 16)) | ((lane >= 37) & (lane < 40)) | (lane >= 61)
        tails.append(jnp.where(edge, shift_x(tail), tail))
    out_ref[:, 256:384] = jnp.where(lane < 64, tails[0], pltpu.roll(tails[1], 64, 1))


def slave_force_kernel(traction_ref, slave_ref, table_ref, own_ref, x_ref, y_ref, xy_ref):
    force = lax.dot_general(
        table_ref[...], traction_ref[...], NN, precision=HIGHEST, preferred_element_type=F32
    )
    pick = onehot(iota((512, 256), 0) == slave_ref[...])
    high, low = split(force)
    element = dot(high, pick, NT) + dot(low, pick, NT)
    own_ref[...] = element[:168]
    x_ref[...] = element[:168, 384:]
    y_ref[...] = element[168:]
    xy_ref[...] = element[168:, 384:]


def assemble_kernel(
    body_ref,
    buffer_ref,
    list_ref,
    list_x_ref,
    list_y_ref,
    list_xy_ref,
    own_ref,
    x_ref,
    y_ref,
    xy_ref,
    spread_ref,
    stack_ref,
    out_ref,
    column_scr,
    place_scr,
):
    on_first = body_ref[0] == 0
    sub = iota((8, 512), 0)
    lists = jnp.zeros((8, 512), jnp.int32)
    for i, ref in enumerate((list_ref, list_x_ref, list_y_ref, list_xy_ref)):
        lists = jnp.where(sub == i, jnp.where(on_first, ref[0], ref[1]), lists)
    column_scr[:, 0:8] = jnp.transpose(lists.astype(F32))
    columns = [
        column_scr[pl.ds(r, 256, stride=2), :][:, 0:8].astype(jnp.int32) for r in range(2)
    ]
    columns = jnp.concatenate(columns, axis=0)
    near = iota((512, 512), 1)
    far = iota((512, 128), 1)
    far = jnp.where(far < 64, far + 448, -1)
    halves = unpack(buffer_ref[...])
    element = []
    for i, rows in ((0, slice(0, 168)), (2, slice(168, 192))):
        data = jnp.concatenate([half[rows] for half in halves], axis=1)
        high, low = split(data)
        inside = onehot(columns[:, i : i + 1] == near)
        outside = onehot(columns[:, i + 1 : i + 2] == far)
        element.append(
            (
                dot(high, inside, NN) + dot(low, inside, NN),
                dot(high, outside, NN) + dot(low, outside, NN),
            )
        )
    inside = jnp.concatenate([element[0][0] + own_ref[...], element[1][0] + y_ref[...]], axis=0)
    outside = jnp.concatenate(
        [
            element[0][1] + pltpu.roll(x_ref[...], 64, 1),
            element[1][1] + pltpu.roll(xy_ref[...], 64, 1),
        ],
        axis=0,
    )
    left = iota((24, 128), 1) < 64
    for la in range(9):
        if la == 8:
            block = outside
        else:
            block = inside[:, 128 * (la // 2) : 128 * (la // 2) + 128]
        for pair in range(4):
            first = block[48 * pair : 48 * pair + 24]
            second = block[48 * pair + 24 : 48 * pair + 48]
            if la % 2 == 0:
                second = pltpu.roll(second, 64, 1)
            else:
                first = pltpu.roll(first, 64, 1)
            place_scr[24 * la : 24 * la + 24, 128 * pair : 128 * pair + 128] = jnp.where(
                left, first, second
            )
    high, low = split(place_scr[...])
    spread = spread_ref[...]
    high, low = split(dot(high, spread, NN) + dot(low, spread, NN))
    stack = stack_ref[...]
    out_ref[...] = dot(stack, high, NN) + dot(stack, low, NN)


def call(kernel, outs, spaces, scratch, name):
    smem = pl.BlockSpec(memory_space=pltpu.SMEM)
    vmem = pl.BlockSpec(memory_space=pltpu.VMEM)
    shapes = [jax.ShapeDtypeStruct(shape, F32) for shape in outs]
    return pl.pallas_call(
        kernel,
        out_shape=shapes if len(shapes) > 1 else shapes[0],
        in_specs=[smem if space == "s" else vmem for space in spaces],
        out_specs=[vmem] * len(shapes) if len(shapes) > 1 else vmem,
        scratch_shapes=[pltpu.VMEM(shape, F32) for shape in scratch],
        name=name,
    )


def cross_body(value):
    return lax.ppermute(value, "body", [(0, 1), (1, 0)])


def across_tiles(buffer):
    return lax.all_to_all(buffer, ("gx", "gy"), split_axis=0, concat_axis=0, tiled=True)


def from_behind(value, by_x, by_y):
    pairs = []
    for x in range(16):
        for y in range(16):
            pairs.append((16 * x + y, 16 * ((x + by_x) % 16) + (y + by_y) % 16))
    return lax.ppermute(value, ("gx", "gy"), pairs)


def local(surface_disp, proj_coords, pair_slave, pair_owner, send_list):
    to_points, to_nodes, spread, stack = tables()
    side = lax.axis_index("body")
    body = side.astype(jnp.int32).reshape(1)
    sign = (2.0 * side.astype(F32) - 1.0).reshape(1)
    surface = surface_disp.reshape(588, 128)
    coords = proj_coords.reshape(2, 36, 2, 128).transpose(1, 2, 0, 3).reshape(144, 128)
    owner = pair_owner.reshape(1, 256)
    outgoing = call(
        gather_kernel, [(256, 384)], "svv", [(256, 512), (2, 512, 128)], "gather"
    )(body, send_list, surface)
    arrived = across_tiles(outgoing)
    packed = call(slave_kernel, [(208, 256)], "vvvvv", [(192, 512)], "slave")(
        surface, pair_slave, coords, owner, to_points
    )
    packed = cross_body(packed)
    list_x = from_behind(send_list, 1, 0)
    list_y = from_behind(send_list, 0, 1)
    list_xy = from_behind(send_list, 1, 1)
    returning, traction = call(
        pair_kernel,
        [(256, 384), (120, 256)],
        "svv",
        [(192, 256), (2, 7, 40, 256), (256, 256)],
        "pairs",
    )(sign, arrived, packed)
    returned = across_tiles(returning)
    own, rim_x, rim_y, rim_xy = call(
        slave_force_kernel,
        [(168, 512), (168, 128), (24, 512), (24, 128)],
        "vvv",
        [],
        "slave_force",
    )(cross_body(traction), pair_slave, to_nodes)
    nodal = call(
        assemble_kernel, [(144, 384)], "s" + "v" * 11, [(512, 128), (216, 512)], "assemble"
    )(
        body,
        returned,
        send_list,
        list_x,
        list_y,
        list_xy,
        own,
        from_behind(rim_x, 1, 0),
        from_behind(rim_y, 0, 1),
        from_behind(rim_xy, 1, 1),
        spread,
        stack,
    )
    return nodal.reshape(1, 3, 48, 384)


def solution(mesh):
    return jax.shard_map(
        local,
        mesh=mesh,
        in_specs=(
            P("body", None, None, ("gx", "gy")),
            P("body", None, None, ("gx", "gy")),
            P("body", ("gx", "gy")),
            P("body", ("gx", "gy"), None),
            P(None, ("gx", "gy"), None),
        ),
        out_specs=P("body", None, "gx", "gy"),
        check_vma=False,
    )
```

time: 204 us -> 119 us (0.58)
  other arithmetic: 44.1 us -> 1.68 us
  local copies, waits for them, and re-layouts: 42.7 us -> 8.57 us
  starting transfers between devices: 37.3 us -> 56.7 us
  matrix products: 17.8 us -> 0 us
  Pallas kernels: 0 us -> 15.4 us
  waiting for transfers between devices: 48 us -> 35.4 us
  blocking collectives: 12.5 us -> 0 us
    scatter-add x5 -> x0, other arithmetic: 33.4 us -> none  [the longest x1 16.7 us: local(): element_force = element_force + jnp.zeros((3, 49, segment_count), jnp.flo...]
    dot_general x4 -> x0, matrix products: 17.8 us -> none  [the longest x1 8.46 us: pair_forces(): jnp.einsum('lqp,cklp->ckqp', second_basis, master_grid, precision=highest)]
    pallas_call x0 -> x5, Pallas kernels: none -> 15.4 us  [the longest x1 4.32 us: local(): call(pair_kernel, [(256, 384), (120, 256)], 'svv', [(192, 256), (2, 7, 40...]
    ppermute x4 -> x8, starting transfers between devices: 9.66 us -> 25 us  [the longest x6 21.2 us: from_behind(): return lax.ppermute(value, ('gx', 'gy'), pairs)]
    all_to_all x1 -> x0, blocking collectives: 12.5 us -> none  [across_tiles(): lax.all_to_all(buffer, 'gx', split_axis=2, concat_axis=2, tiled=True)]
    all_to_all x3 -> x2, waiting for transfers between devices: 37 us -> 25.1 us  [across_tiles(): lax.all_to_all(buffer, ('gx', 'gy'), split_axis=0, concat_axis=0, tiled=T...]
    another operation x11 -> x0, local copies, waits for them, and re-layouts: 10.8 us -> none  [the longest x4 5.46 us: basis_traced(): return jnp.stack(factors)]
    unnamed x20 -> x22, local copies, waits for them, and re-layouts: 12 us -> 3.52 us
  transfers between devices with their start and end apart: 7 -> 10, of which waited for: 6 -> 4; matrix products, arithmetic and copies ran while one was open for 9% -> 1% of each run, Pallas kernels for 0% -> 4%
where the time goes in v1:
time: 119 us; the launch traced here: 118 us
  starting transfers between devices  56.7 us (48%)
  waiting for transfers between devices  35.4 us (30%)
  Pallas kernels  15.4 us (13%)
  local copies, waits for them, and re-layouts  8.57 us (7%)
  other arithmetic  1.68 us (1%)
    all_to_all x2, starting transfers between devices, across_tiles(): lax.all_to_all(buffer, ('gx', 'gy'), split_axis=0, concat_axis=0, tiled=T...  31.6 us
    all_to_all x2, waiting for transfers between devices, across_tiles(): lax.all_to_all(buffer, ('gx', 'gy'), split_axis=0, concat_axis=0, tiled=T...  25.1 us
    ppermute x6, starting transfers between devices, from_behind(): return lax.ppermute(value, ('gx', 'gy'), pairs)  21.2 us
    ppermute x6, waiting for transfers between devices, from_behind(): return lax.ppermute(value, ('gx', 'gy'), pairs)  8.99 us
    pallas_call x1, Pallas kernels, local(): call(pair_kernel, [(256, 384), (120, 256)], 'svv', [(192, 256), (2, 7, 40...  4.32 us
    all_to_all x2, local copies, waits for them, and re-layouts, across_tiles(): lax.all_to_all(buffer, ('gx', 'gy'), split_axis=0, concat_axis=0, tiled=T...  4.3 us
    ppermute x2, starting transfers between devices, cross_body(): return lax.ppermute(value, 'body', [(0, 1), (1, 0)])  3.83 us
    pallas_call x1, Pallas kernels, local(): call(assemble_kernel, [(144, 384)], 's' + 'v' * 11, [(512, 128), (216, 51...  3.67 us
  transfers between devices with their start and end apart: 10, of which 4 were waited for; matrix products, arithmetic and copies ran while one was open for 1% of the time, Pallas kernels for 4%

profile of v1, /device:TPU:64, one launch (start us, length us, event | category | flops | bytes accessed | tf_op | source)
XLA Modules:
  0.0 117.9 jit_solution(12423203404199463358)
XLA Ops:
  0.0 1.7 %reduce = f32[3,49,512]{2,1,0:T(8,128)S(1)} reduce(f32[1,3,49,512]{3,0,2,1:T(1,128)} %param.9, f32[]{:T(128)} %constant.28), dimensions={0}, to_apply=%param.9.reduce_sub_computation | reduce | bytes 602116 | tf_op args[0]
  1.7 0.7 reshape.27.surf_ref
  2.4 2.6 %gather.1 = f32[256,384]{1,0:T(8,128)} custom-call(s32[1]{0:T(128)} %bitcast.body_ref, s32[2,1,512]{2,1,0:T(1,128)} %list_ref.3, f32[588,128]{1,0:T(8,128)} %reshape.27.surf_ref), custom_call_target="tpu_custom_call" | custom-call | tf_op jit(solution)/shard_map/gather/pallas_call | solution.py:420
  5.0 2.1 %copy.11 = f32[256,1,384]{2,1,0:T(1,128)} copy(f32[256,1,384]{2,0,1:T(8,128)} %bitcast.18) | data formatting | bytes 786432 | tf_op jit(solution)/shard_map/all_to_all | solution.py:401
  7.2 22.7 %all-to-all-start = ((f32[256,1,384]{2,1,0:T(1,128)}), f32[256,1,384]{2,1,0:T(1,128)S(1)}, u32[]{:S(2)}, u32[]{:S(2)}) async-start(f32[256,1,384]{2,1,0:T(1,128)} %copy.11), calls=%async_computation | async-start | bytes 786432 | tf_op jit(solution)/shard_map/all_to_all | solution.py:401
  29.8 2.3 %slave.1 = f32[208,256]{1,0:T(8,128)} custom-call(f32[588,128]{1,0:T(8,128)} %reshape.27.surf_ref, s32[1,256]{1,0:T(1,128)} %slave_ref.3, f32[144,128]{1,0:T(8,128)} %bitcast.21, s32[1,256]{1,0:T(1,128)} %bitcast.22, f32[120,192]{1,0:T(8,128)} %constant.19.clone.table_ref), custom_call_target="tpu_custom_call" | custom-call | tf_op jit(solution)/shard_map/slave/pallas_call | solution.py:424
  32.2 1.9 %collective-permute-start = (f32[208,256]{1,0:T(8,128)}, f32[208,256]{1,0:T(8,128)S(1)}, u32[]{:S(2)}, u32[]{:S(2)}) collective-permute-start(f32[208,256]{1,0:T(8,128)} %slave.1), channel_id=1, source_target_pairs={{0,256},{256,0},{1,257},{257,1},{2,258},{258,2},{3,259},{259,3},{4... | collective-permute-start | bytes 638984 | tf_op jit(solution)/shard_map/ppermute | solution.py:397
  34.1 25.1 %all-to-all-done = f32[256,1,384]{2,1,0:T(1,128)S(1)} async-done(((f32[256,1,384]{2,1,0:T(1,128)}), f32[256,1,384]{2,1,0:T(1,128)S(1)}, u32[]{:S(2)}, u32[]{:S(2)}) %all-to-all-start) | async-done | bytes 393248 | tf_op jit(solution)/shard_map/all_to_all | solution.py:401
  59.2 0.8 copy.19
  59.9 0.0 collective-permute-done.pack_ref
  59.9 0.0 copy-start
  60.0 0.7 copy-done
  60.6 4.3 %pairs.1 = (f32[256,384]{1,0:T(8,128)}, f32[120,256]{1,0:T(8,128)}) custom-call(f32[1]{0:T(128)} %bitcast.1.sign_ref, f32[256,384]{1,0:T(8,128)} %bitcast.17, f32[208,256]{1,0:T(8,128)} %copy-done), custom_call_target="tpu_custom_call" | custom-call | tf_op jit(solution)/shard_map/pairs/pallas_call | solution.py:431
  65.0 2.1 %copy.13 = f32[256,1,384]{2,1,0:T(1,128)} copy(f32[256,1,384]{2,0,1:T(8,128)} %bitcast.20) | data formatting | bytes 786432 | tf_op jit(solution)/shard_map/all_to_all | solution.py:401
  67.1 0.0 copy-start.9
  67.1 8.9 %all-to-all-start.1 = ((f32[256,1,384]{2,1,0:T(1,128)}), f32[256,1,384]{2,1,0:T(1,128)S(1)}, u32[]{:S(2)}, u32[]{:S(2)}) async-start(f32[256,1,384]{2,1,0:T(1,128)} %copy.13), calls=%async_computation.1 | async-start | bytes 786432 | tf_op jit(solution)/shard_map/all_to_all | solution.py:401
  76.1 0.0 copy-done.9
  76.1 1.9 %collective-permute-start.4 = (f32[120,256]{1,0:T(8,128)S(1)}, f32[120,256]{1,0:T(8,128)S(1)}, u32[]{:S(2)}, u32[]{:S(2)}) collective-permute-start(f32[120,256]{1,0:T(8,128)S(1)} %copy-done.9), channel_id=1, source_target_pairs={{0,256},{256,0},{1,257},{257,1},{2,258},{258,2},{3,259},{259,3},{4... | collective-permute-start | bytes 368648 | tf_op jit(solution)/shard_map/ppermute | solution.py:397
  78.0 1.3 %collective-permute-done.4.traction_ref = f32[120,256]{1,0:T(8,128)S(1)} collective-permute-done((f32[120,256]{1,0:T(8,128)S(1)}, f32[120,256]{1,0:T(8,128)S(1)}, u32[]{:S(2)}, u32[]{:S(2)}) %collective-permute-start.4) | collective-permute-done | bytes 122912 | tf_op jit(solution)/shard_map/ppermute | solution.py:397
  79.3 0.0 copy-start.1
  79.3 0.6 copy-done.1
  80.0 2.5 %slave_force.1 = (f32[168,512]{1,0:T(8,128)}, f32[168,128]{1,0:T(8,128)}, f32[24,512]{1,0:T(8,128)}, f32[24,128]{1,0:T(8,128)}) custom-call(f32[120,256]{1,0:T(8,128)} %copy-done.1, s32[1,256]{1,0:T(1,128)} %slave_ref.3, f32[192,120]{1,0:T(8,128)} %constant.20.clone.table_ref), custom_call_target="tpu_custom_call" | custom-call | tf_op jit(solution)/shard_map/slave_force/pallas_call | solution.py:439
  82.5 0.0 copy-start.4
  82.5 3.5 %collective-permute-start.5 = (f32[168,128]{1,0:T(8,128)}, f32[168,128]{1,0:T(8,128)S(1)}, u32[]{:S(2)}, u32[]{:S(2)}) collective-permute-start(f32[168,128]{1,0:T(8,128)} %get-tuple-element.14), channel_id=1, source_target_pairs={{0,16},{1,17},{2,18},{3,19},{4,20},{5,21},{6,22},{7,23},{8,24},{9,... | collective-permute-start | bytes 258056 | tf_op jit(solution)/shard_map/ppermute | solution.py:409
  86.0 3.4 %collective-permute-start.6 = (f32[24,512]{1,0:T(8,128)}, f32[24,512]{1,0:T(8,128)S(1)}, u32[]{:S(2)}, u32[]{:S(2)}) collective-permute-start(f32[24,512]{1,0:T(8,128)} %get-tuple-element.15), channel_id=1, source_target_pairs={{0,1},{1,2},{2,3},{3,4},{4,5},{5,6},{6,7},{7,8},{8,9},{9,10},{10,1... | collective-permute-start | bytes 147464 | tf_op jit(solution)/shard_map/ppermute | solution.py:409
  89.4 5.6 %collective-permute-start.7 = (f32[24,128]{1,0:T(8,128)}, f32[24,128]{1,0:T(8,128)S(1)}, u32[]{:S(2)}, u32[]{:S(2)}) collective-permute-start(f32[24,128]{1,0:T(8,128)} %get-tuple-element.16), channel_id=1, source_target_pairs={{0,17},{1,18},{2,19},{3,20},{4,21},{5,22},{6,23},{7,24},{8,25},{9,... | collective-permute-start | bytes 36872 | tf_op jit(solution)/shard_map/ppermute | solution.py:409
  95.0 0.0 copy-done.4
  95.0 3.2 %collective-permute-start.1 = (s32[2,1,512]{2,1,0:T(1,128)S(1)}, s32[2,1,512]{2,1,0:T(1,128)S(1)}, u32[]{:S(2)}, u32[]{:S(2)}) collective-permute-start(s32[2,1,512]{2,1,0:T(1,128)S(1)} %copy-done.4), channel_id=1, source_target_pairs={{0,16},{1,17},{2,18},{3,19},{4,20},{5,21},{6,22},{7,23},{8,24},{9,... | collective-permute-start | bytes 12296 | tf_op jit(solution)/shard_map/ppermute | solution.py:409
  98.2 3.4 %collective-permute-start.2 = (s32[2,1,512]{2,1,0:T(1,128)S(1)}, s32[2,1,512]{2,1,0:T(1,128)S(1)}, u32[]{:S(2)}, u32[]{:S(2)}) collective-permute-start(s32[2,1,512]{2,1,0:T(1,128)S(1)} %copy-done.4), channel_id=1, source_target_pairs={{0,1},{1,2},{2,3},{3,4},{4,5},{5,6},{6,7},{7,8},{8,9},{9,10},{10,1... | collective-permute-start | bytes 12296 | tf_op jit(solution)/shard_map/ppermute | solution.py:409
  101.6 2.2 %collective-permute-done.1.list_x_ref = s32[2,1,512]{2,1,0:T(1,128)S(1)} collective-permute-done((s32[2,1,512]{2,1,0:T(1,128)S(1)}, s32[2,1,512]{2,1,0:T(1,128)S(1)}, u32[]{:S(2)}, u32[]{:S(2)}) %collective-permute-start.1) | collective-permute-done | bytes 4128 | tf_op jit(solution)/shard_map/ppermute | solution.py:409
  103.8 0.0 copy-start.6
  103.8 2.2 %collective-permute-start.3 = (s32[2,1,512]{2,1,0:T(1,128)S(1)}, s32[2,1,512]{2,1,0:T(1,128)S(1)}, u32[]{:S(2)}, u32[]{:S(2)}) collective-permute-start(s32[2,1,512]{2,1,0:T(1,128)S(1)} %copy-done.4), channel_id=1, source_target_pairs={{0,17},{1,18},{2,19},{3,20},{4,21},{5,22},{6,23},{7,24},{8,25},{9,... | collective-permute-start | bytes 12296 | tf_op jit(solution)/shard_map/ppermute | solution.py:409
  106.0 0.0 all-to-all-done.1
  106.0 0.8 copy.18
  106.8 0.0 copy-done.6
  106.8 0.0 collective-permute-done.2.list_y_ref
  106.8 6.7 %collective-permute-done.3.list_xy_ref = s32[2,1,512]{2,1,0:T(1,128)S(1)} collective-permute-done((s32[2,1,512]{2,1,0:T(1,128)S(1)}, s32[2,1,512]{2,1,0:T(1,128)S(1)}, u32[]{:S(2)}, u32[]{:S(2)}) %collective-permute-start.3) | collective-permute-done | bytes 4128 | tf_op jit(solution)/shard_map/ppermute | solution.py:409
  113.5 0.0 collective-permute-done.7.xy_ref
  113.5 0.0 collective-permute-done.6.y_ref
  113.5 0.0 copy-start.3
  113.5 0.0 collective-permute-done.5.x_ref
  113.6 0.0 copy-start.2
  113.6 0.0 copy-done.7
  113.6 0.5 copy-done.8
  114.1 0.0 copy-done.5
  114.1 0.0 copy-done.3
  114.1 0.0 copy-done.2
  114.2 3.7 %assemble.1 = f32[144,384]{1,0:T(8,128)} custom-call(s32[1]{0:T(128)} %bitcast.body_ref, f32[256,384]{1,0:T(8,128)} %bitcast.19, s32[2,1,512]{2,1,0:T(1,128)} %list_ref.3, s32[2,1,512]{2,1,0:T(1,128)} %copy-done.6, s32[2,1,512]{2,1,0:T(1,128)} %copy-done.7, s32[2,1,512]{2,1,0:T(1,128)} %copy-done.8, f32[168,512]{1,0:T(8,128)} %get-tuple-element.13.own_ref, ...), custom_call_target="tpu_custom_call" | custom-call | tf_op jit(solution)/shard_map/assemble/pallas_call | solution.py:446
  (3 shorter events, 0.0 us)
Async XLA Ops:
  7.2 52.0 %all-to-all-start = ((f32[256,1,384]{2,1,0:T(1,128)}), f32[256,1,384]{2,1,0:T(1,128)S(1)}, u32[]{:S(2)}, u32[]{:S(2)}) async-start(f32[256,1,384]{2,1,0:T(1,128)} %copy.11), calls=%async_computation | async-start | bytes 786432 | tf_op jit(solution)/shard_map/all_to_all | solution.py:401
  32.2 27.8 %collective-permute-start = (f32[208,256]{1,0:T(8,128)}, f32[208,256]{1,0:T(8,128)S(1)}, u32[]{:S(2)}, u32[]{:S(2)}) collective-permute-start(f32[208,256]{1,0:T(8,128)} %slave.1), channel_id=1, source_target_pairs={{0,256},{256,0},{1,257},{257,1},{2,258},{258,2},{3,259},{259,3},{4... | collective-permute-start | bytes 638984 | tf_op jit(solution)/shard_map/ppermute | solution.py:397
  59.9 0.7 copy-start
  67.1 9.0 %copy-start.9 = (f32[120,256]{1,0:T(8,128)S(1)}, f32[120,256]{1,0:T(8,128)}, u32[]{:S(2)}) copy-start(f32[120,256]{1,0:T(8,128)} %get-tuple-element.12) | copy-start | bytes 368644
  67.1 38.9 %all-to-all-start.1 = ((f32[256,1,384]{2,1,0:T(1,128)}), f32[256,1,384]{2,1,0:T(1,128)S(1)}, u32[]{:S(2)}, u32[]{:S(2)}) async-start(f32[256,1,384]{2,1,0:T(1,128)} %copy.13), calls=%async_computation.1 | async-start | bytes 786432 | tf_op jit(solution)/shard_map/all_to_all | solution.py:401
  76.1 3.2 %collective-permute-start.4 = (f32[120,256]{1,0:T(8,128)S(1)}, f32[120,256]{1,0:T(8,128)S(1)}, u32[]{:S(2)}, u32[]{:S(2)}) collective-permute-start(f32[120,256]{1,0:T(8,128)S(1)} %copy-done.9), channel_id=1, source_target_pairs={{0,256},{256,0},{1,257},{257,1},{2,258},{258,2},{3,259},{259,3},{4... | collective-permute-start | bytes 368648 | tf_op jit(solution)/shard_map/ppermute | solution.py:397
  79.3 0.6 copy-start.1
  82.5 12.5 %copy-start.4 = (s32[2,1,512]{2,1,0:T(1,128)S(1)}, s32[2,1,512]{2,1,0:T(1,128)}, u32[]{:S(2)}) copy-start(s32[2,1,512]{2,1,0:T(1,128)} %list_ref.3) | copy-start | bytes 12292
  82.5 31.1 %collective-permute-start.5 = (f32[168,128]{1,0:T(8,128)}, f32[168,128]{1,0:T(8,128)S(1)}, u32[]{:S(2)}, u32[]{:S(2)}) collective-permute-start(f32[168,128]{1,0:T(8,128)} %get-tuple-element.14), channel_id=1, source_target_pairs={{0,16},{1,17},{2,18},{3,19},{4,20},{5,21},{6,22},{7,23},{8,24},{9,... | collective-permute-start | bytes 258056 | tf_op jit(solution)/shard_map/ppermute | solution.py:409
  86.0 27.5 %collective-permute-start.6 = (f32[24,512]{1,0:T(8,128)}, f32[24,512]{1,0:T(8,128)S(1)}, u32[]{:S(2)}, u32[]{:S(2)}) collective-permute-start(f32[24,512]{1,0:T(8,128)} %get-tuple-element.15), channel_id=1, source_target_pairs={{0,1},{1,2},{2,3},{3,4},{4,5},{5,6},{6,7},{7,8},{8,9},{9,10},{10,1... | collective-permute-start | bytes 147464 | tf_op jit(solution)/shard_map/ppermute | solution.py:409
  89.4 24.2 %collective-permute-start.7 = (f32[24,128]{1,0:T(8,128)}, f32[24,128]{1,0:T(8,128)S(1)}, u32[]{:S(2)}, u32[]{:S(2)}) collective-permute-start(f32[24,128]{1,0:T(8,128)} %get-tuple-element.16), channel_id=1, source_target_pairs={{0,17},{1,18},{2,19},{3,20},{4,21},{5,22},{6,23},{7,24},{8,25},{9,... | collective-permute-start | bytes 36872 | tf_op jit(solution)/shard_map/ppermute | solution.py:409
  95.0 8.8 %collective-permute-start.1 = (s32[2,1,512]{2,1,0:T(1,128)S(1)}, s32[2,1,512]{2,1,0:T(1,128)S(1)}, u32[]{:S(2)}, u32[]{:S(2)}) collective-permute-start(s32[2,1,512]{2,1,0:T(1,128)S(1)} %copy-done.4), channel_id=1, source_target_pairs={{0,16},{1,17},{2,18},{3,19},{4,20},{5,21},{6,22},{7,23},{8,24},{9,... | collective-permute-start | bytes 12296 | tf_op jit(solution)/shard_map/ppermute | solution.py:409
  98.2 8.6 %collective-permute-start.2 = (s32[2,1,512]{2,1,0:T(1,128)S(1)}, s32[2,1,512]{2,1,0:T(1,128)S(1)}, u32[]{:S(2)}, u32[]{:S(2)}) collective-permute-start(s32[2,1,512]{2,1,0:T(1,128)S(1)} %copy-done.4), channel_id=1, source_target_pairs={{0,1},{1,2},{2,3},{3,4},{4,5},{5,6},{6,7},{7,8},{8,9},{9,10},{10,1... | collective-permute-start | bytes 12296 | tf_op jit(solution)/shard_map/ppermute | solution.py:409
  103.8 3.0 %copy-start.6 = (s32[2,1,512]{2,1,0:T(1,128)}, s32[2,1,512]{2,1,0:T(1,128)S(1)}, u32[]{:S(2)}) copy-start(s32[2,1,512]{2,1,0:T(1,128)S(1)} %collective-permute-done.1.list_x_ref) | copy-start | bytes 12292
  103.8 9.7 %collective-permute-start.3 = (s32[2,1,512]{2,1,0:T(1,128)S(1)}, s32[2,1,512]{2,1,0:T(1,128)S(1)}, u32[]{:S(2)}, u32[]{:S(2)}) collective-permute-start(s32[2,1,512]{2,1,0:T(1,128)S(1)} %copy-done.4), channel_id=1, source_target_pairs={{0,17},{1,18},{2,19},{3,20},{4,21},{5,22},{6,23},{7,24},{8,25},{9,... | collective-permute-start | bytes 12296 | tf_op jit(solution)/shard_map/ppermute | solution.py:409
  106.8 6.8 %copy-start.7 = (s32[2,1,512]{2,1,0:T(1,128)}, s32[2,1,512]{2,1,0:T(1,128)S(1)}, u32[]{:S(2)}) copy-start(s32[2,1,512]{2,1,0:T(1,128)S(1)} %collective-permute-done.2.list_y_ref) | copy-start | bytes 12292
  113.5 0.6 copy-start.8
  113.5 0.6 copy-start.5
  113.5 0.6 copy-start.3
  113.6 0.6 copy-start.2

commit v2 on v1

--- a/solution.py
+++ b/solution.py
@@ -131,10 +131,15 @@
     return lax.broadcasted_iota(jnp.int32, shape, dim)
 
 
+def third(i):
+    return pl.ds(i, 256, stride=3)
+
+
 def load_surface(surf_ref, scratch):
+    flat_ref = surf_ref.reshape(588, 128)
     scratch[144:, :] = jnp.zeros((scratch.shape[0] - 144, 512), F32)
     for j in range(4):
-        scratch[0:147, 128 * j : 128 * j + 128] = surf_ref[pl.ds(j, 147, stride=4), :]
+        scratch[0:147, 128 * j : 128 * j + 128] = flat_ref[pl.ds(j, 147, stride=4), :]
 
 
 def gather_kernel(body_ref, list_ref, surf_ref, out_ref, surf_scr, rows_scr):
@@ -147,9 +152,9 @@
     rows_scr[0] = rows[:, :128]
     rows_scr[1] = rows[:, 128:]
     left = iota((256, 128), 1) < 64
-    out_ref[:, 0:128] = rows_scr[0, pl.ds(0, 256, stride=2), :]
-    out_ref[:, 128:256] = rows_scr[0, pl.ds(1, 256, stride=2), :]
-    out_ref[:, 256:384] = jnp.where(
+    out_ref[third(0), :] = rows_scr[0, pl.ds(0, 256, stride=2), :]
+    out_ref[third(1), :] = rows_scr[0, pl.ds(1, 256, stride=2), :]
+    out_ref[third(2), :] = jnp.where(
         left,
         rows_scr[1, pl.ds(0, 256, stride=2), :],
         pltpu.roll(rows_scr[1, pl.ds(1, 256, stride=2), :], 64, 1),
@@ -170,11 +175,13 @@
             out_ref[120 + 40 * e : 156 + 40 * e, 128 * j : 128 * j + 128] = coord_ref[
                 pl.ds(2 * j + e, 36, stride=4), :
             ]
-    out_ref[200:208, :] = jnp.broadcast_to(owner_ref[...].astype(F32), (8, 256))
-
-
-def unpack(buffer):
-    turned = [jnp.transpose(buffer[:, 128 * i : 128 * i + 128]) for i in range(3)]
+    out_ref[200:208, :] = jnp.where(
+        iota((8, 256), 0) == 0, owner_ref[...], slave_ref[...]
+    ).astype(F32)
+
+
+def unpack(buffer_ref):
+    turned = [jnp.transpose(buffer_ref[third(i), :]) for i in range(3)]
     return (
         jnp.concatenate([turned[0], turned[2][:64]], axis=0),
         jnp.concatenate([turned[1], turned[2][64:]], axis=0),
@@ -192,7 +199,7 @@
     before = dot(pick, earlier, NN)
     picks = [onehot(named & (before < 0.5)), onehot(named & (before > 0.5))]
     master = jnp.zeros((192, 256), F32)
-    for half, chosen in zip(unpack(buffer_ref[...]), picks):
+    for half, chosen in zip(unpack(buffer_ref), picks):
         high, low = split(half)
         master = master + dot(high, chosen, NN) + dot(low, chosen, NN)
     master_scr[...] = master
@@ -284,19 +291,19 @@
     tails = []
     for r in range(2):
         head = to_owner[r][:, :128]
-        out_ref[:, 128 * r : 128 * r + 128] = jnp.where(rim, shift_x(head), head)
+        out_ref[third(r), :] = jnp.where(rim, shift_x(head), head)
         tail = to_owner[r][:, 128:]
         tail = jnp.where(lane >= 40, shift_y(tail), tail)
         edge = ((lane >= 13) & (lane < 16)) | ((lane >= 37) & (lane < 40)) | (lane >= 61)
         tails.append(jnp.where(edge, shift_x(tail), tail))
-    out_ref[:, 256:384] = jnp.where(lane < 64, tails[0], pltpu.roll(tails[1], 64, 1))
-
-
-def slave_force_kernel(traction_ref, slave_ref, table_ref, own_ref, x_ref, y_ref, xy_ref):
+    out_ref[third(2), :] = jnp.where(lane < 64, tails[0], pltpu.roll(tails[1], 64, 1))
+
+
+def slave_force_kernel(traction_ref, pack_ref, table_ref, own_ref, x_ref, y_ref, xy_ref):
     force = lax.dot_general(
         table_ref[...], traction_ref[...], NN, precision=HIGHEST, preferred_element_type=F32
     )
-    pick = onehot(iota((512, 256), 0) == slave_ref[...])
+    pick = onehot(iota((512, 256), 0) == pack_ref[201:202, :].astype(jnp.int32))
     high, low = split(force)
     element = dot(high, pick, NT) + dot(low, pick, NT)
     own_ref[...] = element[:168]
@@ -305,13 +312,22 @@
     xy_ref[...] = element[168:, 384:]
 
 
+def column_kernel(
+    body_ref, list_ref, list_x_ref, list_y_ref, list_xy_ref, out_ref, column_scr
+):
+    on_first = body_ref[0] == 0
+    sub = iota((8, 512), 0)
+    lists = jnp.zeros((8, 512), jnp.int32)
+    for i, ref in enumerate((list_ref, list_x_ref, list_y_ref, list_xy_ref)):
+        lists = jnp.where(sub == i, jnp.where(on_first, ref[0], ref[1]), lists)
+    column_scr[:, 0:8] = jnp.transpose(lists.astype(F32))
+    for r in range(2):
+        out_ref[256 * r : 256 * r + 256, :] = column_scr[pl.ds(r, 256, stride=2), :]
+
+
 def assemble_kernel(
-    body_ref,
     buffer_ref,
-    list_ref,
-    list_x_ref,
-    list_y_ref,
-    list_xy_ref,
+    column_ref,
     own_ref,
     x_ref,
     y_ref,
@@ -319,23 +335,13 @@
     spread_ref,
     stack_ref,
     out_ref,
-    column_scr,
     place_scr,
 ):
-    on_first = body_ref[0] == 0
-    sub = iota((8, 512), 0)
-    lists = jnp.zeros((8, 512), jnp.int32)
-    for i, ref in enumerate((list_ref, list_x_ref, list_y_ref, list_xy_ref)):
-        lists = jnp.where(sub == i, jnp.where(on_first, ref[0], ref[1]), lists)
-    column_scr[:, 0:8] = jnp.transpose(lists.astype(F32))
-    columns = [
-        column_scr[pl.ds(r, 256, stride=2), :][:, 0:8].astype(jnp.int32) for r in range(2)
-    ]
-    columns = jnp.concatenate(columns, axis=0)
+    columns = column_ref[:, 0:8].astype(jnp.int32)
     near = iota((512, 512), 1)
     far = iota((512, 128), 1)
     far = jnp.where(far < 64, far + 448, -1)
-    halves = unpack(buffer_ref[...])
+    halves = unpack(buffer_ref)
     element = []
     for i, rows in ((0, slice(0, 168)), (2, slice(168, 192))):
         data = jnp.concatenate([half[rows] for half in halves], axis=1)
@@ -382,8 +388,10 @@
 def call(kernel, outs, spaces, scratch, name):
     smem = pl.BlockSpec(memory_space=pltpu.SMEM)
     vmem = pl.BlockSpec(memory_space=pltpu.VMEM)
-    shapes = [jax.ShapeDtypeStruct(shape, F32) for shape in outs]
-    return pl.pallas_call(
+    shapes = [pltpu.VMEM(shape, F32) for shape in outs]
+    if name == "assemble":
+        shapes = [jax.ShapeDtypeStruct(outs[0], F32)]
+    run = pl.pallas_call(
         kernel,
         out_shape=shapes if len(shapes) > 1 else shapes[0],
         in_specs=[smem if space == "s" else vmem for space in spaces],
@@ -392,21 +400,31 @@
         name=name,
     )
 
-
-def cross_body(value):
-    return lax.ppermute(value, "body", [(0, 1), (1, 0)])
-
-
-def across_tiles(buffer):
-    return lax.all_to_all(buffer, ("gx", "gy"), split_axis=0, concat_axis=0, tiled=True)
-
-
-def from_behind(value, by_x, by_y):
+    def placed(*operands):
+        return run(
+            *[
+                value if space == "s" else pltpu.with_memory_space_constraint(value, pltpu.VMEM)
+                for space, value in zip(spaces, operands)
+            ]
+        )
+
+    return placed
+
+
+def shifted(value, swap, by_x, by_y):
     pairs = []
-    for x in range(16):
-        for y in range(16):
-            pairs.append((16 * x + y, 16 * ((x + by_x) % 16) + (y + by_y) % 16))
-    return lax.ppermute(value, ("gx", "gy"), pairs)
+    for b in range(2):
+        for x in range(16):
+            for y in range(16):
+                to = 256 * (b ^ swap) + 16 * ((x + by_x) % 16) + (y + by_y) % 16
+                pairs.append((256 * b + 16 * x + y, to))
+    return lax.ppermute(value, ("body", "gx", "gy"), pairs)
+
+
+def across_tiles(rows):
+    buffer = rows.reshape(256, 3, 1, 128).transpose(0, 2, 1, 3).reshape(256, 1, 384)
+    buffer = lax.all_to_all(buffer, ("gx", "gy"), split_axis=0, concat_axis=0, tiled=True)
+    return buffer.reshape(256, 1, 3, 128).transpose(0, 2, 1, 3).reshape(768, 128)
 
 
 def local(surface_disp, proj_coords, pair_slave, pair_owner, send_list):
@@ -414,23 +432,28 @@
     side = lax.axis_index("body")
     body = side.astype(jnp.int32).reshape(1)
     sign = (2.0 * side.astype(F32) - 1.0).reshape(1)
-    surface = surface_disp.reshape(588, 128)
+    surface = surface_disp.reshape(147, 1, 512)
     coords = proj_coords.reshape(2, 36, 2, 128).transpose(1, 2, 0, 3).reshape(144, 128)
     owner = pair_owner.reshape(1, 256)
     outgoing = call(
-        gather_kernel, [(256, 384)], "svv", [(256, 512), (2, 512, 128)], "gather"
+        gather_kernel, [(768, 128)], "svv", [(256, 512), (2, 512, 128)], "gather"
     )(body, send_list, surface)
     arrived = across_tiles(outgoing)
     packed = call(slave_kernel, [(208, 256)], "vvvvv", [(192, 512)], "slave")(
         surface, pair_slave, coords, owner, to_points
     )
-    packed = cross_body(packed)
-    list_x = from_behind(send_list, 1, 0)
-    list_y = from_behind(send_list, 0, 1)
-    list_xy = from_behind(send_list, 1, 1)
+    packed = shifted(packed, 1, 0, 0)
+    columns = call(column_kernel, [(512, 128)], "svvvv", [(512, 128)], "columns")(
+        body,
+        send_list,
+        shifted(send_list, 0, 1, 0),
+        shifted(send_list, 0, 0, 1),
+        shifted(send_list, 0, 1, 1),
+    )
+    packed, columns = lax.optimization_barrier((packed, columns))
     returning, traction = call(
         pair_kernel,
-        [(256, 384), (120, 256)],
+        [(768, 128), (120, 256)],
         "svv",
         [(192, 256), (2, 7, 40, 256), (256, 256)],
         "pairs",
@@ -442,20 +465,14 @@
         "vvv",
         [],
         "slave_force",
-    )(cross_body(traction), pair_slave, to_nodes)
-    nodal = call(
-        assemble_kernel, [(144, 384)], "s" + "v" * 11, [(512, 128), (216, 512)], "assemble"
-    )(
-        body,
+    )(traction, packed, to_nodes)
+    nodal = call(assemble_kernel, [(144, 384)], "v" * 8, [(216, 512)], "assemble")(
         returned,
-        send_list,
-        list_x,
-        list_y,
-        list_xy,
-        own,
-        from_behind(rim_x, 1, 0),
-        from_behind(rim_y, 0, 1),
-        from_behind(rim_xy, 1, 1),
+        columns,
+        shifted(own, 1, 0, 0),
+        shifted(rim_x, 1, 1, 0),
+        shifted(rim_y, 1, 0, 1),
+        shifted(rim_xy, 1, 1, 1),
         spread,
         stack,
     )

time: 119 us -> 101 us (0.85)
  the two profiles are of different devices: /device:TPU:64 before, /device:TPU:8 now
where the time goes in v2:
time: 101 us; the launch traced here: 100 us
  starting transfers between devices  59.2 us (59%)
  waiting for transfers between devices  29.8 us (30%)
  Pallas kernels  8.6 us (9%)
  local copies, waits for them, and re-layouts  2.31 us (2%)
    all_to_all x2, starting transfers between devices, across_tiles(): lax.all_to_all(buffer, ('gx', 'gy'), split_axis=0, concat_axis=0, tiled=T...  33 us
    ppermute x8, starting transfers between devices, shifted(): return lax.ppermute(value, ('body', 'gx', 'gy'), pairs)  26.2 us
    all_to_all x2, waiting for transfers between devices, across_tiles(): lax.all_to_all(buffer, ('gx', 'gy'), split_axis=0, concat_axis=0, tiled=T...  19.1 us
    ppermute x8, waiting for transfers between devices, shifted(): return lax.ppermute(value, ('body', 'gx', 'gy'), pairs)  10.7 us
    pallas_call x6, Pallas kernels, placed(): run(*[value if space == 's' else pltpu.with_memory_space_constraint(value...  8.6 us
    unnamed x20, local copies, waits for them, and re-layouts  2.31 us
  transfers between devices with their start and end apart: 10, of which 5 were waited for; matrix products, arithmetic and copies ran while one was open for 0% of the time, Pallas kernels for 2%

profile of v2, /device:TPU:8, one launch (start us, length us, event | category | flops | bytes accessed | tf_op | source)
XLA Modules:
  0.0 100.1 jit_solution(16724085604396426210)
XLA Ops:
  0.0 0.0 copy-start.7
  0.0 0.7 copy-done.7
  0.7 0.0 copy-start
  0.7 1.0 copy-done
  1.7 1.6 %gather.1 = f32[768,128]{1,0:T(8,128)} custom-call(s32[1]{0:T(128)} %bitcast.1.body_ref, s32[2,1,512]{2,1,0:T(1,128)S(1)} %copy-done.7, f32[147,1,512]{2,1,0:T(1,128)S(1)} %bitcast.16), custom_call_target="tpu_custom_call" | custom-call | tf_op jit(solution)/shard_map/gather/pallas_call | solution.py:404
  3.2 0.0 copy-start.1
  3.3 0.0 copy-start.3
  3.3 0.0 copy-start.6
  3.3 0.0 copy-start.9
  3.3 23.9 %all-to-all-start = ((f32[256,1,384]{2,1,0:T(1,128)}), f32[256,1,384]{2,1,0:T(1,128)S(1)}, u32[]{:S(2)}, u32[]{:S(2)}) async-start(f32[256,1,384]{2,1,0:T(1,128)} %bitcast.3), calls=%async_computation | async-start | bytes 786432 | tf_op jit(solution)/shard_map/all_to_all | solution.py:426
  27.2 0.0 copy-start.8
  27.2 0.0 copy-done.1
  27.2 0.0 copy-done.3
  27.2 0.0 copy-done.6
  27.2 0.0 copy-done.9
  27.3 0.6 copy-done.8
  27.9 0.6 slave.1
  28.5 1.9 %collective-permute-start = (f32[208,256]{1,0:T(8,128)S(1)}, f32[208,256]{1,0:T(8,128)S(1)}, u32[]{:S(2)}, u32[]{:S(2)}) collective-permute-start(f32[208,256]{1,0:T(8,128)S(1)} %slave.1), channel_id=1, source_target_pairs={{0,256},{1,257},{2,258},{3,259},{4,260},{5,261},{6,262},{7,263},{8... | collective-permute-start | bytes 638984 | tf_op jit(solution)/shard_map/ppermute | solution.py:421
  30.4 3.4 %collective-permute-start.2 = (s32[2,1,512]{2,1,0:T(1,128)S(1)}, s32[2,1,512]{2,1,0:T(1,128)S(1)}, u32[]{:S(2)}, u32[]{:S(2)}) collective-permute-start(s32[2,1,512]{2,1,0:T(1,128)S(1)} %copy-done.7), channel_id=1, source_target_pairs={{0,1},{1,2},{2,3},{3,4},{4,5},{5,6},{6,7},{7,8},{8,9},{9,10},{10,1... | collective-permute-start | bytes 12296 | tf_op jit(solution)/shard_map/ppermute | solution.py:421
  33.8 3.5 %collective-permute-start.1 = (s32[2,1,512]{2,1,0:T(1,128)S(1)}, s32[2,1,512]{2,1,0:T(1,128)S(1)}, u32[]{:S(2)}, u32[]{:S(2)}) collective-permute-start(s32[2,1,512]{2,1,0:T(1,128)S(1)} %copy-done.7), channel_id=1, source_target_pairs={{0,16},{1,17},{2,18},{3,19},{4,20},{5,21},{6,22},{7,23},{8,24},{9,... | collective-permute-start | bytes 12296 | tf_op jit(solution)/shard_map/ppermute | solution.py:421
  37.3 4.4 %collective-permute-start.3 = (s32[2,1,512]{2,1,0:T(1,128)S(1)}, s32[2,1,512]{2,1,0:T(1,128)S(1)}, u32[]{:S(2)}, u32[]{:S(2)}) collective-permute-start(s32[2,1,512]{2,1,0:T(1,128)S(1)} %copy-done.7), channel_id=1, source_target_pairs={{0,17},{1,18},{2,19},{3,20},{4,21},{5,22},{6,23},{7,24},{8,25},{9,... | collective-permute-start | bytes 12296 | tf_op jit(solution)/shard_map/ppermute | solution.py:421
  41.7 1.9 %collective-permute-done.2.list_y_ref = s32[2,1,512]{2,1,0:T(1,128)S(1)} collective-permute-done((s32[2,1,512]{2,1,0:T(1,128)S(1)}, s32[2,1,512]{2,1,0:T(1,128)S(1)}, u32[]{:S(2)}, u32[]{:S(2)}) %collective-permute-start.2) | collective-permute-done | bytes 4128 | tf_op jit(solution)/shard_map/ppermute | solution.py:421
  43.5 0.0 collective-permute-done.1.list_x_ref
  43.5 3.5 %collective-permute-done.3.list_xy_ref = s32[2,1,512]{2,1,0:T(1,128)S(1)} collective-permute-done((s32[2,1,512]{2,1,0:T(1,128)S(1)}, s32[2,1,512]{2,1,0:T(1,128)S(1)}, u32[]{:S(2)}, u32[]{:S(2)}) %collective-permute-start.3) | collective-permute-done | bytes 4128 | tf_op jit(solution)/shard_map/ppermute | solution.py:421
  47.0 0.2 columns.1.column_ref
  47.2 0.0 collective-permute-done.pack_ref
  47.2 9.4 %all-to-all-done = f32[256,1,384]{2,1,0:T(1,128)S(1)} async-done(((f32[256,1,384]{2,1,0:T(1,128)}), f32[256,1,384]{2,1,0:T(1,128)S(1)}, u32[]{:S(2)}, u32[]{:S(2)}) %all-to-all-start) | async-done | bytes 393248 | tf_op jit(solution)/shard_map/all_to_all | solution.py:426
  56.6 3.3 %pairs.1 = (f32[768,128]{1,0:T(8,128)}, f32[120,256]{1,0:T(8,128)S(1)}) custom-call(f32[1]{0:T(128)} %bitcast.sign_ref, f32[768,128]{1,0:T(8,128)S(1)} %bitcast.14, f32[208,256]{1,0:T(8,128)S(1)} %collective-permute-done.pack_ref), custom_call_target="tpu_custom_call" | custom-call | tf_op jit(solution)/shard_map/pairs/pallas_call | solution.py:404
  59.9 0.0 copy-start.4
  59.9 0.0 copy-start.5
  59.9 9.1 %all-to-all-start.1 = ((f32[256,1,384]{2,1,0:T(1,128)}), f32[256,1,384]{2,1,0:T(1,128)S(1)}, u32[]{:S(2)}, u32[]{:S(2)}) async-start(f32[256,1,384]{2,1,0:T(1,128)} %bitcast.9), calls=%async_computation.1 | async-start | bytes 786432 | tf_op jit(solution)/shard_map/all_to_all | solution.py:426
  68.9 0.0 copy-start.2
  69.0 0.0 copy-done.4
  69.0 0.8 slave_force.1
  69.7 1.9 %collective-permute-start.4 = (f32[168,512]{1,0:T(8,128)S(1)}, f32[168,512]{1,0:T(8,128)S(1)}, u32[]{:S(2)}, u32[]{:S(2)}) collective-permute-start(f32[168,512]{1,0:T(8,128)S(1)} %get-tuple-element.17), channel_id=1, source_target_pairs={{0,256},{1,257},{2,258},{3,259},{4,260},{5,261},{6,262},{7,263},{8... | collective-permute-start | bytes 1032200 | tf_op jit(solution)/shard_map/ppermute | solution.py:421
  71.7 3.6 %collective-permute-start.5 = (f32[168,128]{1,0:T(8,128)S(1)}, f32[168,128]{1,0:T(8,128)S(1)}, u32[]{:S(2)}, u32[]{:S(2)}) collective-permute-start(f32[168,128]{1,0:T(8,128)S(1)} %get-tuple-element.18), channel_id=1, source_target_pairs={{0,272},{1,273},{2,274},{3,275},{4,276},{5,277},{6,278},{7,279},{8... | collective-permute-start | bytes 258056 | tf_op jit(solution)/shard_map/ppermute | solution.py:421
  75.3 3.0 %collective-permute-start.6 = (f32[24,512]{1,0:T(8,128)S(1)}, f32[24,512]{1,0:T(8,128)S(1)}, u32[]{:S(2)}, u32[]{:S(2)}) collective-permute-start(f32[24,512]{1,0:T(8,128)S(1)} %get-tuple-element.19), channel_id=1, source_target_pairs={{0,257},{1,258},{2,259},{3,260},{4,261},{5,262},{6,263},{7,264},{8... | collective-permute-start | bytes 147464 | tf_op jit(solution)/shard_map/ppermute | solution.py:421
  78.3 4.5 %collective-permute-start.7 = (f32[24,128]{1,0:T(8,128)S(1)}, f32[24,128]{1,0:T(8,128)S(1)}, u32[]{:S(2)}, u32[]{:S(2)}) collective-permute-start(f32[24,128]{1,0:T(8,128)S(1)} %get-tuple-element.20), channel_id=1, source_target_pairs={{0,273},{1,274},{2,275},{3,276},{4,277},{5,278},{6,279},{7,280},{8... | collective-permute-start | bytes 36872 | tf_op jit(solution)/shard_map/ppermute | solution.py:421
  82.8 5.4 %collective-permute-done.7.xy_ref = f32[24,128]{1,0:T(8,128)S(1)} collective-permute-done((f32[24,128]{1,0:T(8,128)S(1)}, f32[24,128]{1,0:T(8,128)S(1)}, u32[]{:S(2)}, u32[]{:S(2)}) %collective-permute-start.7) | collective-permute-done | bytes 12320 | tf_op jit(solution)/shard_map/ppermute | solution.py:421
  88.1 0.0 collective-permute-done.6.y_ref
  88.1 0.0 collective-permute-done.5.x_ref
  88.1 0.0 collective-permute-done.4.own_ref
  88.1 9.7 %all-to-all-done.1 = f32[256,1,384]{2,1,0:T(1,128)S(1)} async-done(((f32[256,1,384]{2,1,0:T(1,128)}), f32[256,1,384]{2,1,0:T(1,128)S(1)}, u32[]{:S(2)}, u32[]{:S(2)}) %all-to-all-start.1) | async-done | bytes 393248 | tf_op jit(solution)/shard_map/all_to_all | solution.py:426
  97.9 0.0 copy-done.5
  97.9 0.0 copy-done.2
  97.9 2.2 %assemble.1 = f32[144,384]{1,0:T(8,128)} custom-call(f32[768,128]{1,0:T(8,128)S(1)} %bitcast.15, f32[512,128]{1,0:T(8,128)S(1)} %columns.1.column_ref, f32[168,512]{1,0:T(8,128)S(1)} %collective-permute-done.4.own_ref, f32[168,128]{1,0:T(8,128)S(1)} %collective-permute-done.5.x_ref, f32[24,512]{1,0:T(8,128)S(1)} %collective-permute-done.6.y_ref, ...), custom_call_target="tpu_custom_call" | custom-call | tf_op jit(solution)/shard_map/assemble/pallas_call | solution.py:404
Async XLA Ops:
  0.0 0.7 copy-start.7
  0.7 1.0 copy-start
  3.2 24.0 %copy-start.1 = (f32[1,3,49,512]{3,0,2,1:T(1,128)S(1)}, f32[1,3,49,512]{3,0,2,1:T(1,128)}, u32[]{:S(2)}) copy-start(f32[1,3,49,512]{3,0,2,1:T(1,128)} %param.9) | copy-start | bytes 903172
  3.3 24.0 %copy-start.3 = (f32[120,192]{1,0:T(8,128)S(1)}, f32[120,192]{1,0:T(8,128)}, u32[]{:S(2)}) copy-start(f32[120,192]{1,0:T(8,128)} %constant.19.clone.table_ref) | copy-start | bytes 276484
  3.3 24.0 %copy-start.6 = (f32[1,2,36,256]{3,1,2,0:T(2,128)S(1)}, f32[1,2,36,256]{3,1,2,0:T(2,128)}, u32[]{:S(2)}) copy-start(f32[1,2,36,256]{3,1,2,0:T(2,128)} %param.10) | copy-start | bytes 221188
  3.3 24.0 %copy-start.9 = (s32[1,256,1]{1,2,0:T(1,128)S(1)}, s32[1,256,1]{1,2,0:T(1,128)}, u32[]{:S(2)}) copy-start(s32[1,256,1]{1,2,0:T(1,128)} %param.12) | copy-start | bytes 3076
  3.3 53.3 %all-to-all-start = ((f32[256,1,384]{2,1,0:T(1,128)}), f32[256,1,384]{2,1,0:T(1,128)S(1)}, u32[]{:S(2)}, u32[]{:S(2)}) async-start(f32[256,1,384]{2,1,0:T(1,128)} %bitcast.3), calls=%async_computation | async-start | bytes 786432 | tf_op jit(solution)/shard_map/all_to_all | solution.py:426
  27.2 0.7 copy-start.8
  28.5 18.7 %collective-permute-start = (f32[208,256]{1,0:T(8,128)S(1)}, f32[208,256]{1,0:T(8,128)S(1)}, u32[]{:S(2)}, u32[]{:S(2)}) collective-permute-start(f32[208,256]{1,0:T(8,128)S(1)} %slave.1), channel_id=1, source_target_pairs={{0,256},{1,257},{2,258},{3,259},{4,260},{5,261},{6,262},{7,263},{8... | collective-permute-start | bytes 638984 | tf_op jit(solution)/shard_map/ppermute | solution.py:421
  30.4 13.1 %collective-permute-start.2 = (s32[2,1,512]{2,1,0:T(1,128)S(1)}, s32[2,1,512]{2,1,0:T(1,128)S(1)}, u32[]{:S(2)}, u32[]{:S(2)}) collective-permute-start(s32[2,1,512]{2,1,0:T(1,128)S(1)} %copy-done.7), channel_id=1, source_target_pairs={{0,1},{1,2},{2,3},{3,4},{4,5},{5,6},{6,7},{7,8},{8,9},{9,10},{10,1... | collective-permute-start | bytes 12296 | tf_op jit(solution)/shard_map/ppermute | solution.py:421
  33.8 9.8 %collective-permute-start.1 = (s32[2,1,512]{2,1,0:T(1,128)S(1)}, s32[2,1,512]{2,1,0:T(1,128)S(1)}, u32[]{:S(2)}, u32[]{:S(2)}) collective-permute-start(s32[2,1,512]{2,1,0:T(1,128)S(1)} %copy-done.7), channel_id=1, source_target_pairs={{0,16},{1,17},{2,18},{3,19},{4,20},{5,21},{6,22},{7,23},{8,24},{9,... | collective-permute-start | bytes 12296 | tf_op jit(solution)/shard_map/ppermute | solution.py:421
  37.3 9.7 %collective-permute-start.3 = (s32[2,1,512]{2,1,0:T(1,128)S(1)}, s32[2,1,512]{2,1,0:T(1,128)S(1)}, u32[]{:S(2)}, u32[]{:S(2)}) collective-permute-start(s32[2,1,512]{2,1,0:T(1,128)S(1)} %copy-done.7), channel_id=1, source_target_pairs={{0,17},{1,18},{2,19},{3,20},{4,21},{5,22},{6,23},{7,24},{8,25},{9,... | collective-permute-start | bytes 12296 | tf_op jit(solution)/shard_map/ppermute | solution.py:421
  59.9 9.1 %copy-start.4 = (f32[192,120]{1,0:T(8,128)S(1)}, f32[192,120]{1,0:T(8,128)}, u32[]{:S(2)}) copy-start(f32[192,120]{1,0:T(8,128)} %constant.20.clone.table_ref) | copy-start | bytes 276484
  59.9 38.0 %copy-start.5 = (bf16[144,216]{1,0:T(8,128)(2,1)S(1)}, bf16[144,216]{1,0:T(8,128)(2,1)}, u32[]{:S(2)}) copy-start(bf16[144,216]{1,0:T(8,128)(2,1)} %constant.22.clone.stack_ref) | copy-start | bytes 186628
  59.9 38.0 %all-to-all-start.1 = ((f32[256,1,384]{2,1,0:T(1,128)}), f32[256,1,384]{2,1,0:T(1,128)S(1)}, u32[]{:S(2)}, u32[]{:S(2)}) async-start(f32[256,1,384]{2,1,0:T(1,128)} %bitcast.9), calls=%async_computation.1 | async-start | bytes 786432 | tf_op jit(solution)/shard_map/all_to_all | solution.py:426
  68.9 28.9 %copy-start.2 = (bf16[512,384]{1,0:T(8,128)(2,1)S(1)}, bf16[512,384]{1,0:T(8,128)(2,1)}, u32[]{:S(2)}) copy-start(bf16[512,384]{1,0:T(8,128)(2,1)} %constant.21.clone.spread_ref) | copy-start | bytes 1179652
  69.7 18.4 %collective-permute-start.4 = (f32[168,512]{1,0:T(8,128)S(1)}, f32[168,512]{1,0:T(8,128)S(1)}, u32[]{:S(2)}, u32[]{:S(2)}) collective-permute-start(f32[168,512]{1,0:T(8,128)S(1)} %get-tuple-element.17), channel_id=1, source_target_pairs={{0,256},{1,257},{2,258},{3,259},{4,260},{5,261},{6,262},{7,263},{8... | collective-permute-start | bytes 1032200 | tf_op jit(solution)/shard_map/ppermute | solution.py:421
  71.7 16.5 %collective-permute-start.5 = (f32[168,128]{1,0:T(8,128)S(1)}, f32[168,128]{1,0:T(8,128)S(1)}, u32[]{:S(2)}, u32[]{:S(2)}) collective-permute-start(f32[168,128]{1,0:T(8,128)S(1)} %get-tuple-element.18), channel_id=1, source_target_pairs={{0,272},{1,273},{2,274},{3,275},{4,276},{5,277},{6,278},{7,279},{8... | collective-permute-start | bytes 258056 | tf_op jit(solution)/shard_map/ppermute | solution.py:421
  75.3 12.9 %collective-permute-start.6 = (f32[24,512]{1,0:T(8,128)S(1)}, f32[24,512]{1,0:T(8,128)S(1)}, u32[]{:S(2)}, u32[]{:S(2)}) collective-permute-start(f32[24,512]{1,0:T(8,128)S(1)} %get-tuple-element.19), channel_id=1, source_target_pairs={{0,257},{1,258},{2,259},{3,260},{4,261},{5,262},{6,263},{7,264},{8... | collective-permute-start | bytes 147464 | tf_op jit(solution)/shard_map/ppermute | solution.py:421
  78.3 9.9 %collective-permute-start.7 = (f32[24,128]{1,0:T(8,128)S(1)}, f32[24,128]{1,0:T(8,128)S(1)}, u32[]{:S(2)}, u32[]{:S(2)}) collective-permute-start(f32[24,128]{1,0:T(8,128)S(1)} %get-tuple-element.20), channel_id=1, source_target_pairs={{0,273},{1,274},{2,275},{3,276},{4,277},{5,278},{6,279},{7,280},{8... | collective-permute-start | bytes 36872 | tf_op jit(solution)/shard_map/ppermute | solution.py:421

commit v3 on v2

--- a/solution.py
+++ b/solution.py
@@ -188,21 +188,14 @@
     )
 
 
-def pair_kernel(
-    sign_ref, buffer_ref, pack_ref, out_ref, traction_ref, master_scr, basis_scr, force_scr
-):
-    sign = sign_ref[0]
+def prepare_kernel(pack_ref, basis_ref, pick_ref):
     owner = pack_ref[200:201, :].astype(jnp.int32)
     named = owner == iota((256, 256), 0)
     pick = onehot(named)
     earlier = onehot(iota((256, 256), 0) < iota((256, 256), 1))
     before = dot(pick, earlier, NN)
-    picks = [onehot(named & (before < 0.5)), onehot(named & (before > 0.5))]
-    master = jnp.zeros((192, 256), F32)
-    for half, chosen in zip(unpack(buffer_ref), picks):
-        high, low = split(half)
-        master = master + dot(high, chosen, NN) + dot(low, chosen, NN)
-    master_scr[...] = master
+    pick_ref[0] = onehot(named & (before < 0.5))
+    pick_ref[1] = onehot(named & (before > 0.5))
     scales = lagrange_scales()
     for e in range(2):
         coord = pack_ref[120 + 40 * e : 160 + 40 * e, :]
@@ -221,7 +214,27 @@
                 value = prefix[6]
             else:
                 value = prefix[k] * suffix[k]
-            basis_scr[e, k] = value * scales[k]
+            basis_ref[e, k] = value * scales[k]
+
+
+def pair_kernel(
+    sign_ref,
+    buffer_ref,
+    pack_ref,
+    basis_scr,
+    pick_ref,
+    out_ref,
+    traction_ref,
+    master_scr,
+    force_scr,
+):
+    sign = sign_ref[0]
+    picks = [pick_ref[0], pick_ref[1]]
+    master = jnp.zeros((192, 256), F32)
+    for half, chosen in zip(unpack(buffer_ref), picks):
+        high, low = split(half)
+        master = master + dot(high, chosen, NN) + dot(low, chosen, NN)
+    master_scr[...] = master
     point = iota((8, 128), 0)
     for t in range(5):
         q = point + 8 * t
@@ -385,10 +398,10 @@
     out_ref[...] = dot(stack, high, NN) + dot(stack, low, NN)
 
 
-def call(kernel, outs, spaces, scratch, name):
+def call(kernel, outs, spaces, scratch, name, types=None):
     smem = pl.BlockSpec(memory_space=pltpu.SMEM)
     vmem = pl.BlockSpec(memory_space=pltpu.VMEM)
-    shapes = [pltpu.VMEM(shape, F32) for shape in outs]
+    shapes = [pltpu.VMEM(shape, dtype) for shape, dtype in zip(outs, types or [F32] * len(outs))]
     if name == "assemble":
         shapes = [jax.ShapeDtypeStruct(outs[0], F32)]
     run = pl.pallas_call(
@@ -403,7 +416,7 @@
     def placed(*operands):
         return run(
             *[
-                value if space == "s" else pltpu.with_memory_space_constraint(value, pltpu.VMEM)
+                value if space == "s" or name == "gather" else pltpu.with_memory_space_constraint(value, pltpu.VMEM)
                 for space, value in zip(spaces, operands)
             ]
         )
@@ -450,14 +463,22 @@
         shifted(send_list, 0, 0, 1),
         shifted(send_list, 0, 1, 1),
     )
-    packed, columns = lax.optimization_barrier((packed, columns))
+    basis, picks = call(
+        prepare_kernel,
+        [(2, 7, 40, 256), (2, 256, 256)],
+        "v",
+        [],
+        "prepare",
+        [F32, BF16],
+    )(packed)
+    basis, columns = lax.optimization_barrier((basis, columns))
     returning, traction = call(
         pair_kernel,
         [(768, 128), (120, 256)],
-        "svv",
-        [(192, 256), (2, 7, 40, 256), (256, 256)],
+        "svvvv",
+        [(192, 256), (256, 256)],
         "pairs",
-    )(sign, arrived, packed)
+    )(sign, arrived, packed, basis, picks)
     returned = across_tiles(returning)
     own, rim_x, rim_y, rim_xy = call(
         slave_force_kernel,

time: 101 us -> 99.5 us (0.985)
  local copies, waits for them, and re-layouts: 2.31 us -> 0.67 us
    unnamed x20 -> x18, local copies, waits for them, and re-layouts: 2.31 us -> 0.67 us
    pallas_call x6 -> x7, Pallas kernels: 8.6 us -> 9.33 us  [placed(): run(*[value if space == 's' or name == 'gather' else pltpu.with_memory_sp...]
where the time goes in v3:
time: 99.5 us; the launch traced here: 98.9 us
  starting transfers between devices  59.2 us (59%)
  waiting for transfers between devices  29.6 us (30%)
  Pallas kernels  9.33 us (9%)
    all_to_all x2, starting transfers between devices, across_tiles(): lax.all_to_all(buffer, ('gx', 'gy'), split_axis=0, concat_axis=0, tiled=T...  33 us
    ppermute x8, starting transfers between devices, shifted(): return lax.ppermute(value, ('body', 'gx', 'gy'), pairs)  26.2 us
    all_to_all x2, waiting for transfers between devices, across_tiles(): lax.all_to_all(buffer, ('gx', 'gy'), split_axis=0, concat_axis=0, tiled=T...  19 us
    ppermute x8, waiting for transfers between devices, shifted(): return lax.ppermute(value, ('body', 'gx', 'gy'), pairs)  10.6 us
    pallas_call x7, Pallas kernels, placed(): run(*[value if space == 's' or name == 'gather' else pltpu.with_memory_sp...  9.33 us
  transfers between devices with their start and end apart: 10, of which 5 were waited for; matrix products, arithmetic and copies ran while one was open for 0% of the time, Pallas kernels for 2%

profile of v3, /device:TPU:8, one launch (start us, length us, event | category | flops | bytes accessed | tf_op | source)
XLA Modules:
  0.0 98.9 jit_solution(16044861796896647613)
XLA Ops:
  0.0 2.6 %gather.1 = f32[768,128]{1,0:T(8,128)} custom-call(s32[1]{0:T(128)} %bitcast.1.body_ref, s32[2,1,512]{2,1,0:T(1,128)} %list_ref.3, f32[147,1,512]{2,1,0:T(1,128)} %bitcast.16), custom_call_target="tpu_custom_call" | custom-call | tf_op jit(solution)/shard_map/gather/pallas_call | solution.py:417
  2.6 0.0 copy-start
  2.6 0.0 copy-start.2
  2.6 0.0 copy-start.5
  2.6 0.0 copy-start.8
  2.6 23.9 %all-to-all-start = ((f32[256,1,384]{2,1,0:T(1,128)}), f32[256,1,384]{2,1,0:T(1,128)S(1)}, u32[]{:S(2)}, u32[]{:S(2)}) async-start(f32[256,1,384]{2,1,0:T(1,128)} %bitcast.3), calls=%async_computation | async-start | bytes 786432 | tf_op jit(solution)/shard_map/all_to_all | solution.py:439
  26.5 0.0 copy-start.7
  26.6 0.0 copy-done
  26.6 0.0 copy-done.2
  26.6 0.0 copy-done.5
  26.6 0.0 copy-done.8
  26.6 0.6 copy-done.7
  27.2 0.0 copy-start.6
  27.2 0.6 slave.1
  27.8 1.9 %collective-permute-start = (f32[208,256]{1,0:T(8,128)S(1)}, f32[208,256]{1,0:T(8,128)S(1)}, u32[]{:S(2)}, u32[]{:S(2)}) collective-permute-start(f32[208,256]{1,0:T(8,128)S(1)} %slave.1), channel_id=1, source_target_pairs={{0,256},{1,257},{2,258},{3,259},{4,260},{5,261},{6,262},{7,263},{8... | collective-permute-start | bytes 638984 | tf_op jit(solution)/shard_map/ppermute | solution.py:434
  29.7 0.0 copy-done.6
  29.7 3.4 %collective-permute-start.2 = (s32[2,1,512]{2,1,0:T(1,128)S(1)}, s32[2,1,512]{2,1,0:T(1,128)S(1)}, u32[]{:S(2)}, u32[]{:S(2)}) collective-permute-start(s32[2,1,512]{2,1,0:T(1,128)S(1)} %copy-done.6), channel_id=1, source_target_pairs={{0,1},{1,2},{2,3},{3,4},{4,5},{5,6},{6,7},{7,8},{8,9},{9,10},{10,1... | collective-permute-start | bytes 12296 | tf_op jit(solution)/shard_map/ppermute | solution.py:434
  33.1 3.5 %collective-permute-start.1 = (s32[2,1,512]{2,1,0:T(1,128)S(1)}, s32[2,1,512]{2,1,0:T(1,128)S(1)}, u32[]{:S(2)}, u32[]{:S(2)}) collective-permute-start(s32[2,1,512]{2,1,0:T(1,128)S(1)} %copy-done.6), channel_id=1, source_target_pairs={{0,16},{1,17},{2,18},{3,19},{4,20},{5,21},{6,22},{7,23},{8,24},{9,... | collective-permute-start | bytes 12296 | tf_op jit(solution)/shard_map/ppermute | solution.py:434
  36.6 4.4 %collective-permute-start.3 = (s32[2,1,512]{2,1,0:T(1,128)S(1)}, s32[2,1,512]{2,1,0:T(1,128)S(1)}, u32[]{:S(2)}, u32[]{:S(2)}) collective-permute-start(s32[2,1,512]{2,1,0:T(1,128)S(1)} %copy-done.6), channel_id=1, source_target_pairs={{0,17},{1,18},{2,19},{3,20},{4,21},{5,22},{6,23},{7,24},{8,25},{9,... | collective-permute-start | bytes 12296 | tf_op jit(solution)/shard_map/ppermute | solution.py:434
  41.0 1.9 %collective-permute-done.2.list_y_ref = s32[2,1,512]{2,1,0:T(1,128)S(1)} collective-permute-done((s32[2,1,512]{2,1,0:T(1,128)S(1)}, s32[2,1,512]{2,1,0:T(1,128)S(1)}, u32[]{:S(2)}, u32[]{:S(2)}) %collective-permute-start.2) | collective-permute-done | bytes 4128 | tf_op jit(solution)/shard_map/ppermute | solution.py:434
  42.9 0.0 collective-permute-done.1.list_x_ref
  42.9 3.5 %collective-permute-done.3.list_xy_ref = s32[2,1,512]{2,1,0:T(1,128)S(1)} collective-permute-done((s32[2,1,512]{2,1,0:T(1,128)S(1)}, s32[2,1,512]{2,1,0:T(1,128)S(1)}, u32[]{:S(2)}, u32[]{:S(2)}) %collective-permute-start.3) | collective-permute-done | bytes 4128 | tf_op jit(solution)/shard_map/ppermute | solution.py:434
  46.3 0.2 columns.1.column_ref
  46.5 0.0 collective-permute-done.pack_ref
  46.5 0.3 prepare.1
  46.8 9.1 %all-to-all-done = f32[256,1,384]{2,1,0:T(1,128)S(1)} async-done(((f32[256,1,384]{2,1,0:T(1,128)}), f32[256,1,384]{2,1,0:T(1,128)S(1)}, u32[]{:S(2)}, u32[]{:S(2)}) %all-to-all-start) | async-done | bytes 393248 | tf_op jit(solution)/shard_map/all_to_all | solution.py:439
  55.9 2.7 %pairs.1 = (f32[768,128]{1,0:T(8,128)}, f32[120,256]{1,0:T(8,128)S(1)}) custom-call(f32[1]{0:T(128)} %bitcast.sign_ref, f32[768,128]{1,0:T(8,128)S(1)} %bitcast.15, f32[208,256]{1,0:T(8,128)S(1)} %collective-permute-done.pack_ref, f32[2,7,40,256]{3,2,1,0:T(8,128)S(1)} %get-tuple-element.16.basis_scr, bf16[2,256,256]{2,1,0:T(8,128)(2,1)S(1)} %get-tuple-element.17.pick_ref), custom_call_target="tpu_custom_call" | custom-call | tf_op jit(solution)/shard_map/pairs/pallas_call | solution.py:417
  58.6 0.0 copy-start.3
  58.6 0.0 copy-start.4
  58.6 9.1 %all-to-all-start.1 = ((f32[256,1,384]{2,1,0:T(1,128)}), f32[256,1,384]{2,1,0:T(1,128)S(1)}, u32[]{:S(2)}, u32[]{:S(2)}) async-start(f32[256,1,384]{2,1,0:T(1,128)} %bitcast.9), calls=%async_computation.1 | async-start | bytes 786432 | tf_op jit(solution)/shard_map/all_to_all | solution.py:439
  67.7 0.0 copy-start.1
  67.7 0.0 copy-done.3
  67.7 0.8 slave_force.1
  68.5 1.9 %collective-permute-start.4 = (f32[168,512]{1,0:T(8,128)S(1)}, f32[168,512]{1,0:T(8,128)S(1)}, u32[]{:S(2)}, u32[]{:S(2)}) collective-permute-start(f32[168,512]{1,0:T(8,128)S(1)} %get-tuple-element.21), channel_id=1, source_target_pairs={{0,256},{1,257},{2,258},{3,259},{4,260},{5,261},{6,262},{7,263},{8... | collective-permute-start | bytes 1032200 | tf_op jit(solution)/shard_map/ppermute | solution.py:434
  70.4 3.6 %collective-permute-start.5 = (f32[168,128]{1,0:T(8,128)S(1)}, f32[168,128]{1,0:T(8,128)S(1)}, u32[]{:S(2)}, u32[]{:S(2)}) collective-permute-start(f32[168,128]{1,0:T(8,128)S(1)} %get-tuple-element.22), channel_id=1, source_target_pairs={{0,272},{1,273},{2,274},{3,275},{4,276},{5,277},{6,278},{7,279},{8... | collective-permute-start | bytes 258056 | tf_op jit(solution)/shard_map/ppermute | solution.py:434
  74.0 3.0 %collective-permute-start.6 = (f32[24,512]{1,0:T(8,128)S(1)}, f32[24,512]{1,0:T(8,128)S(1)}, u32[]{:S(2)}, u32[]{:S(2)}) collective-permute-start(f32[24,512]{1,0:T(8,128)S(1)} %get-tuple-element.23), channel_id=1, source_target_pairs={{0,257},{1,258},{2,259},{3,260},{4,261},{5,262},{6,263},{7,264},{8... | collective-permute-start | bytes 147464 | tf_op jit(solution)/shard_map/ppermute | solution.py:434
  77.0 4.5 %collective-permute-start.7 = (f32[24,128]{1,0:T(8,128)S(1)}, f32[24,128]{1,0:T(8,128)S(1)}, u32[]{:S(2)}, u32[]{:S(2)}) collective-permute-start(f32[24,128]{1,0:T(8,128)S(1)} %get-tuple-element.24), channel_id=1, source_target_pairs={{0,273},{1,274},{2,275},{3,276},{4,277},{5,278},{6,279},{7,280},{8... | collective-permute-start | bytes 36872 | tf_op jit(solution)/shard_map/ppermute | solution.py:434
  81.5 5.2 %collective-permute-done.7.xy_ref = f32[24,128]{1,0:T(8,128)S(1)} collective-permute-done((f32[24,128]{1,0:T(8,128)S(1)}, f32[24,128]{1,0:T(8,128)S(1)}, u32[]{:S(2)}, u32[]{:S(2)}) %collective-permute-start.7) | collective-permute-done | bytes 12320 | tf_op jit(solution)/shard_map/ppermute | solution.py:434
  86.7 0.0 collective-permute-done.6.y_ref
  86.7 0.0 collective-permute-done.5.x_ref
  86.7 0.0 collective-permute-done.4.own_ref
  86.8 10.0 %all-to-all-done.1 = f32[256,1,384]{2,1,0:T(1,128)S(1)} async-done(((f32[256,1,384]{2,1,0:T(1,128)}), f32[256,1,384]{2,1,0:T(1,128)S(1)}, u32[]{:S(2)}, u32[]{:S(2)}) %all-to-all-start.1) | async-done | bytes 393248 | tf_op jit(solution)/shard_map/all_to_all | solution.py:439
  96.7 0.0 copy-done.4
  96.7 0.0 copy-done.1
  96.7 2.2 %assemble.1 = f32[144,384]{1,0:T(8,128)} custom-call(f32[768,128]{1,0:T(8,128)S(1)} %bitcast.14, f32[512,128]{1,0:T(8,128)S(1)} %columns.1.column_ref, f32[168,512]{1,0:T(8,128)S(1)} %collective-permute-done.4.own_ref, f32[168,128]{1,0:T(8,128)S(1)} %collective-permute-done.5.x_ref, f32[24,512]{1,0:T(8,128)S(1)} %collective-permute-done.6.y_ref, ...), custom_call_target="tpu_custom_call" | custom-call | tf_op jit(solution)/shard_map/assemble/pallas_call | solution.py:417
Async XLA Ops:
  2.6 24.0 %copy-start = (f32[1,3,49,512]{3,0,2,1:T(1,128)S(1)}, f32[1,3,49,512]{3,0,2,1:T(1,128)}, u32[]{:S(2)}) copy-start(f32[1,3,49,512]{3,0,2,1:T(1,128)} %param.9) | copy-start | bytes 903172
  2.6 24.0 %copy-start.2 = (f32[120,192]{1,0:T(8,128)S(1)}, f32[120,192]{1,0:T(8,128)}, u32[]{:S(2)}) copy-start(f32[120,192]{1,0:T(8,128)} %constant.19.clone.table_ref) | copy-start | bytes 276484
  2.6 24.0 %copy-start.5 = (f32[1,2,36,256]{3,1,2,0:T(2,128)S(1)}, f32[1,2,36,256]{3,1,2,0:T(2,128)}, u32[]{:S(2)}) copy-start(f32[1,2,36,256]{3,1,2,0:T(2,128)} %param.10) | copy-start | bytes 221188
  2.6 24.0 %copy-start.8 = (s32[1,256,1]{1,2,0:T(1,128)S(1)}, s32[1,256,1]{1,2,0:T(1,128)}, u32[]{:S(2)}) copy-start(s32[1,256,1]{1,2,0:T(1,128)} %param.12) | copy-start | bytes 3076
  2.6 53.3 %all-to-all-start = ((f32[256,1,384]{2,1,0:T(1,128)}), f32[256,1,384]{2,1,0:T(1,128)S(1)}, u32[]{:S(2)}, u32[]{:S(2)}) async-start(f32[256,1,384]{2,1,0:T(1,128)} %bitcast.3), calls=%async_computation | async-start | bytes 786432 | tf_op jit(solution)/shard_map/all_to_all | solution.py:439
  26.5 0.7 copy-start.7
  27.2 2.5 %copy-start.6 = (s32[2,1,512]{2,1,0:T(1,128)S(1)}, s32[2,1,512]{2,1,0:T(1,128)}, u32[]{:S(2)}) copy-start(s32[2,1,512]{2,1,0:T(1,128)} %list_ref.3) | copy-start | bytes 12292
  27.8 18.7 %collective-permute-start = (f32[208,256]{1,0:T(8,128)S(1)}, f32[208,256]{1,0:T(8,128)S(1)}, u32[]{:S(2)}, u32[]{:S(2)}) collective-permute-start(f32[208,256]{1,0:T(8,128)S(1)} %slave.1), channel_id=1, source_target_pairs={{0,256},{1,257},{2,258},{3,259},{4,260},{5,261},{6,262},{7,263},{8... | collective-permute-start | bytes 638984 | tf_op jit(solution)/shard_map/ppermute | solution.py:434
  29.7 13.1 %collective-permute-start.2 = (s32[2,1,512]{2,1,0:T(1,128)S(1)}, s32[2,1,512]{2,1,0:T(1,128)S(1)}, u32[]{:S(2)}, u32[]{:S(2)}) collective-permute-start(s32[2,1,512]{2,1,0:T(1,128)S(1)} %copy-done.6), channel_id=1, source_target_pairs={{0,1},{1,2},{2,3},{3,4},{4,5},{5,6},{6,7},{7,8},{8,9},{9,10},{10,1... | collective-permute-start | bytes 12296 | tf_op jit(solution)/shard_map/ppermute | solution.py:434
  33.1 9.7 %collective-permute-start.1 = (s32[2,1,512]{2,1,0:T(1,128)S(1)}, s32[2,1,512]{2,1,0:T(1,128)S(1)}, u32[]{:S(2)}, u32[]{:S(2)}) collective-permute-start(s32[2,1,512]{2,1,0:T(1,128)S(1)} %copy-done.6), channel_id=1, source_target_pairs={{0,16},{1,17},{2,18},{3,19},{4,20},{5,21},{6,22},{7,23},{8,24},{9,... | collective-permute-start | bytes 12296 | tf_op jit(solution)/shard_map/ppermute | solution.py:434
  36.6 9.7 %collective-permute-start.3 = (s32[2,1,512]{2,1,0:T(1,128)S(1)}, s32[2,1,512]{2,1,0:T(1,128)S(1)}, u32[]{:S(2)}, u32[]{:S(2)}) collective-permute-start(s32[2,1,512]{2,1,0:T(1,128)S(1)} %copy-done.6), channel_id=1, source_target_pairs={{0,17},{1,18},{2,19},{3,20},{4,21},{5,22},{6,23},{7,24},{8,25},{9,... | collective-permute-start | bytes 12296 | tf_op jit(solution)/shard_map/ppermute | solution.py:434
  58.6 9.1 %copy-start.3 = (f32[192,120]{1,0:T(8,128)S(1)}, f32[192,120]{1,0:T(8,128)}, u32[]{:S(2)}) copy-start(f32[192,120]{1,0:T(8,128)} %constant.20.clone.table_ref) | copy-start | bytes 276484
  58.6 38.1 %copy-start.4 = (bf16[144,216]{1,0:T(8,128)(2,1)S(1)}, bf16[144,216]{1,0:T(8,128)(2,1)}, u32[]{:S(2)}) copy-start(bf16[144,216]{1,0:T(8,128)(2,1)} %constant.22.clone.stack_ref) | copy-start | bytes 186628
  58.6 38.1 %all-to-all-start.1 = ((f32[256,1,384]{2,1,0:T(1,128)}), f32[256,1,384]{2,1,0:T(1,128)S(1)}, u32[]{:S(2)}, u32[]{:S(2)}) async-start(f32[256,1,384]{2,1,0:T(1,128)} %bitcast.9), calls=%async_computation.1 | async-start | bytes 786432 | tf_op jit(solution)/shard_map/all_to_all | solution.py:439
  67.7 29.0 %copy-start.1 = (bf16[512,384]{1,0:T(8,128)(2,1)S(1)}, bf16[512,384]{1,0:T(8,128)(2,1)}, u32[]{:S(2)}) copy-start(bf16[512,384]{1,0:T(8,128)(2,1)} %constant.21.clone.spread_ref) | copy-start | bytes 1179652
  68.5 18.2 %collective-permute-start.4 = (f32[168,512]{1,0:T(8,128)S(1)}, f32[168,512]{1,0:T(8,128)S(1)}, u32[]{:S(2)}, u32[]{:S(2)}) collective-permute-start(f32[168,512]{1,0:T(8,128)S(1)} %get-tuple-element.21), channel_id=1, source_target_pairs={{0,256},{1,257},{2,258},{3,259},{4,260},{5,261},{6,262},{7,263},{8... | collective-permute-start | bytes 1032200 | tf_op jit(solution)/shard_map/ppermute | solution.py:434
  70.4 16.3 %collective-permute-start.5 = (f32[168,128]{1,0:T(8,128)S(1)}, f32[168,128]{1,0:T(8,128)S(1)}, u32[]{:S(2)}, u32[]{:S(2)}) collective-permute-start(f32[168,128]{1,0:T(8,128)S(1)} %get-tuple-element.22), channel_id=1, source_target_pairs={{0,272},{1,273},{2,274},{3,275},{4,276},{5,277},{6,278},{7,279},{8... | collective-permute-start | bytes 258056 | tf_op jit(solution)/shard_map/ppermute | solution.py:434
  74.0 12.7 %collective-permute-start.6 = (f32[24,512]{1,0:T(8,128)S(1)}, f32[24,512]{1,0:T(8,128)S(1)}, u32[]{:S(2)}, u32[]{:S(2)}) collective-permute-start(f32[24,512]{1,0:T(8,128)S(1)} %get-tuple-element.23), channel_id=1, source_target_pairs={{0,257},{1,258},{2,259},{3,260},{4,261},{5,262},{6,263},{7,264},{8... | collective-permute-start | bytes 147464 | tf_op jit(solution)/shard_map/ppermute | solution.py:434
  77.0 9.7 %collective-permute-start.7 = (f32[24,128]{1,0:T(8,128)S(1)}, f32[24,128]{1,0:T(8,128)S(1)}, u32[]{:S(2)}, u32[]{:S(2)}) collective-permute-start(f32[24,128]{1,0:T(8,128)S(1)} %get-tuple-element.24), channel_id=1, source_target_pairs={{0,273},{1,274},{2,275},{3,276},{4,277},{5,278},{6,279},{7,280},{8... | collective-permute-start | bytes 36872 | tf_op jit(solution)/shard_map/ppermute | solution.py:434

commit v4 on v3

--- a/solution.py
+++ b/solution.py
@@ -312,7 +312,16 @@
     out_ref[third(2), :] = jnp.where(lane < 64, tails[0], pltpu.roll(tails[1], 64, 1))
 
 
-def slave_force_kernel(traction_ref, pack_ref, table_ref, own_ref, x_ref, y_ref, xy_ref):
+def slave_force_kernel(
+    traction_ref, pack_ref, table_ref, column_ref, own_ref, x_ref, y_ref, xy_ref, hot_ref
+):
+    columns = column_ref[:, 0:8].astype(jnp.int32)
+    near = iota((512, 512), 1)
+    far = iota((512, 128), 1)
+    far = jnp.where(far < 64, far + 448, -1)
+    for i in (0, 2):
+        hot_ref[:, 320 * i : 320 * i + 512] = onehot(columns[:, i : i + 1] == near)
+        hot_ref[:, 320 * i + 512 : 320 * i + 640] = onehot(columns[:, i + 1 : i + 2] == far)
     force = lax.dot_general(
         table_ref[...], traction_ref[...], NN, precision=HIGHEST, preferred_element_type=F32
     )
@@ -340,7 +349,7 @@
 
 def assemble_kernel(
     buffer_ref,
-    column_ref,
+    hot_ref,
     own_ref,
     x_ref,
     y_ref,
@@ -350,17 +359,13 @@
     out_ref,
     place_scr,
 ):
-    columns = column_ref[:, 0:8].astype(jnp.int32)
-    near = iota((512, 512), 1)
-    far = iota((512, 128), 1)
-    far = jnp.where(far < 64, far + 448, -1)
     halves = unpack(buffer_ref)
     element = []
     for i, rows in ((0, slice(0, 168)), (2, slice(168, 192))):
         data = jnp.concatenate([half[rows] for half in halves], axis=1)
         high, low = split(data)
-        inside = onehot(columns[:, i : i + 1] == near)
-        outside = onehot(columns[:, i + 1 : i + 2] == far)
+        inside = hot_ref[:, 320 * i : 320 * i + 512]
+        outside = hot_ref[:, 320 * i + 512 : 320 * i + 640]
         element.append(
             (
                 dot(high, inside, NN) + dot(low, inside, NN),
@@ -480,16 +485,17 @@
         "pairs",
     )(sign, arrived, packed, basis, picks)
     returned = across_tiles(returning)
-    own, rim_x, rim_y, rim_xy = call(
+    own, rim_x, rim_y, rim_xy, hot = call(
         slave_force_kernel,
-        [(168, 512), (168, 128), (24, 512), (24, 128)],
-        "vvv",
+        [(168, 512), (168, 128), (24, 512), (24, 128), (512, 1280)],
+        "vvvv",
         [],
         "slave_force",
-    )(traction, packed, to_nodes)
+        [F32, F32, F32, F32, BF16],
+    )(traction, packed, to_nodes, columns)
     nodal = call(assemble_kernel, [(144, 384)], "v" * 8, [(216, 512)], "assemble")(
         returned,
-        columns,
+        hot,
         shifted(own, 1, 0, 0),
         shifted(rim_x, 1, 1, 0),
         shifted(rim_y, 1, 0, 1),

time: 99.5 us -> 102 us (1.025)
  local copies, waits for them, and re-layouts: 0.67 us -> 5.17 us
  waiting for transfers between devices: 29.6 us -> 28.4 us
    unnamed x18 -> x22, local copies, waits for them, and re-layouts: 0.67 us -> 5.17 us
where the time goes in v4:
time: 102 us
  starting transfers between devices  58.7 us (58%)
  waiting for transfers between devices  28.4 us (28%)
  Pallas kernels  9.24 us (9%)
  local copies, waits for them, and re-layouts  5.17 us (5%)
    all_to_all x2, starting transfers between devices, across_tiles(): lax.all_to_all(buffer, ('gx', 'gy'), split_axis=0, concat_axis=0, tiled=T...  32.6 us
    ppermute x8, starting transfers between devices, shifted(): return lax.ppermute(value, ('body', 'gx', 'gy'), pairs)  26.1 us
    all_to_all x2, waiting for transfers between devices, across_tiles(): lax.all_to_all(buffer, ('gx', 'gy'), split_axis=0, concat_axis=0, tiled=T...  18.1 us
    ppermute x8, waiting for transfers between devices, shifted(): return lax.ppermute(value, ('body', 'gx', 'gy'), pairs)  10.3 us
    pallas_call x7, Pallas kernels, placed(): run(*[value if space == 's' or name == 'gather' else pltpu.with_memory_sp...  9.24 us
    unnamed x22, local copies, waits for them, and re-layouts  5.17 us
  transfers between devices with their start and end apart: 10, of which 5 were waited for; matrix products, arithmetic and copies ran while one was open for 0% of the time, Pallas kernels for 2%

profile of v4, /device:TPU:8, one launch (start us, length us, event | category | flops | bytes accessed | tf_op | source)
XLA Modules:
  0.0 101.7 jit_solution(5961846410462416784)
XLA Ops:
  0.0 0.0 copy-start.4
  0.0 0.0 copy-start.8
  0.0 0.0 copy-start.2
  0.0 0.0 copy-start.10
  0.0 0.0 copy-start.9
  0.0 0.0 copy-start.7
  0.0 2.6 %gather.1 = f32[768,128]{1,0:T(8,128)} custom-call(s32[1]{0:T(128)} %bitcast.1.body_ref, s32[2,1,512]{2,1,0:T(1,128)} %list_ref.3, f32[147,1,512]{2,1,0:T(1,128)} %bitcast.16), custom_call_target="tpu_custom_call" | custom-call | tf_op jit(solution)/shard_map/gather/pallas_call | solution.py:422
  2.7 23.8 %all-to-all-start = ((f32[256,1,384]{2,1,0:T(1,128)}), f32[256,1,384]{2,1,0:T(1,128)S(1)}, u32[]{:S(2)}, u32[]{:S(2)}) async-start(f32[256,1,384]{2,1,0:T(1,128)} %bitcast.3), calls=%async_computation | async-start | bytes 786432 | tf_op jit(solution)/shard_map/all_to_all | solution.py:444
  26.5 0.0 copy-done.4
  26.5 0.0 copy-done.2
  26.5 0.0 copy-done.10
  26.5 0.0 copy-done.9
  26.5 0.0 copy-done.7
  26.5 0.6 slave.1
  27.1 1.9 %collective-permute-start = (f32[208,256]{1,0:T(8,128)S(1)}, f32[208,256]{1,0:T(8,128)S(1)}, u32[]{:S(2)}, u32[]{:S(2)}) collective-permute-start(f32[208,256]{1,0:T(8,128)S(1)} %slave.1), channel_id=1, source_target_pairs={{0,256},{1,257},{2,258},{3,259},{4,260},{5,261},{6,262},{7,263},{8... | collective-permute-start | bytes 638984 | tf_op jit(solution)/shard_map/ppermute | solution.py:439
  29.0 0.0 copy-done.8
  29.0 3.4 %collective-permute-start.2 = (s32[2,1,512]{2,1,0:T(1,128)S(1)}, s32[2,1,512]{2,1,0:T(1,128)S(1)}, u32[]{:S(2)}, u32[]{:S(2)}) collective-permute-start(s32[2,1,512]{2,1,0:T(1,128)S(1)} %copy-done.8), channel_id=1, source_target_pairs={{0,1},{1,2},{2,3},{3,4},{4,5},{5,6},{6,7},{7,8},{8,9},{9,10},{10,1... | collective-permute-start | bytes 12296 | tf_op jit(solution)/shard_map/ppermute | solution.py:439
  32.4 3.5 %collective-permute-start.1 = (s32[2,1,512]{2,1,0:T(1,128)S(1)}, s32[2,1,512]{2,1,0:T(1,128)S(1)}, u32[]{:S(2)}, u32[]{:S(2)}) collective-permute-start(s32[2,1,512]{2,1,0:T(1,128)S(1)} %copy-done.8), channel_id=1, source_target_pairs={{0,16},{1,17},{2,18},{3,19},{4,20},{5,21},{6,22},{7,23},{8,24},{9,... | collective-permute-start | bytes 12296 | tf_op jit(solution)/shard_map/ppermute | solution.py:439
  35.9 4.4 %collective-permute-start.3 = (s32[2,1,512]{2,1,0:T(1,128)S(1)}, s32[2,1,512]{2,1,0:T(1,128)S(1)}, u32[]{:S(2)}, u32[]{:S(2)}) collective-permute-start(s32[2,1,512]{2,1,0:T(1,128)S(1)} %copy-done.8), channel_id=1, source_target_pairs={{0,17},{1,18},{2,19},{3,20},{4,21},{5,22},{6,23},{7,24},{8,25},{9,... | collective-permute-start | bytes 12296 | tf_op jit(solution)/shard_map/ppermute | solution.py:439
  40.3 2.6 %collective-permute-done.2.list_y_ref = s32[2,1,512]{2,1,0:T(1,128)S(1)} collective-permute-done((s32[2,1,512]{2,1,0:T(1,128)S(1)}, s32[2,1,512]{2,1,0:T(1,128)S(1)}, u32[]{:S(2)}, u32[]{:S(2)}) %collective-permute-start.2) | collective-permute-done | bytes 4128 | tf_op jit(solution)/shard_map/ppermute | solution.py:439
  42.9 0.0 collective-permute-done.1.list_x_ref
  42.9 2.9 %collective-permute-done.3.list_xy_ref = s32[2,1,512]{2,1,0:T(1,128)S(1)} collective-permute-done((s32[2,1,512]{2,1,0:T(1,128)S(1)}, s32[2,1,512]{2,1,0:T(1,128)S(1)}, u32[]{:S(2)}, u32[]{:S(2)}) %collective-permute-start.3) | collective-permute-done | bytes 4128 | tf_op jit(solution)/shard_map/ppermute | solution.py:439
  45.8 0.2 columns.1.column_ref
  46.0 0.0 collective-permute-done.pack_ref
  46.0 0.3 prepare.1
  46.3 9.6 %all-to-all-done = f32[256,1,384]{2,1,0:T(1,128)S(1)} async-done(((f32[256,1,384]{2,1,0:T(1,128)}), f32[256,1,384]{2,1,0:T(1,128)S(1)}, u32[]{:S(2)}, u32[]{:S(2)}) %all-to-all-start) | async-done | bytes 393248 | tf_op jit(solution)/shard_map/all_to_all | solution.py:444
  55.9 2.7 %pairs.1 = (f32[768,128]{1,0:T(8,128)}, f32[120,256]{1,0:T(8,128)S(1)}) custom-call(f32[1]{0:T(128)} %bitcast.sign_ref, f32[768,128]{1,0:T(8,128)S(1)} %bitcast.14, f32[208,256]{1,0:T(8,128)S(1)} %collective-permute-done.pack_ref, f32[2,7,40,256]{3,2,1,0:T(8,128)S(1)} %get-tuple-element.17.basis_scr, bf16[2,256,256]{2,1,0:T(8,128)(2,1)S(1)} %get-tuple-element.18.pick_ref), custom_call_target="tpu_custom_call" | custom-call | tf_op jit(solution)/shard_map/pairs/pallas_call | solution.py:422
  58.6 8.8 %all-to-all-start.1 = ((f32[256,1,384]{2,1,0:T(1,128)}), f32[256,1,384]{2,1,0:T(1,128)S(1)}, u32[]{:S(2)}, u32[]{:S(2)}) async-start(f32[256,1,384]{2,1,0:T(1,128)} %bitcast.9), calls=%async_computation.1 | async-start | bytes 786432 | tf_op jit(solution)/shard_map/all_to_all | solution.py:444
  67.4 0.0 copy-start.5
  67.4 0.9 copy-done.5
  68.3 0.8 slave_force.1
  69.1 0.0 copy-start
  69.1 1.1 %copy-done = bf16[512,1280]{1,0:T(8,128)(2,1)} copy-done((bf16[512,1280]{1,0:T(8,128)(2,1)}, bf16[512,1280]{1,0:T(8,128)(2,1)S(1)}, u32[]{:S(2)}) %copy-start) | copy-done | bytes 1310744
  70.2 1.9 %collective-permute-start.4 = (f32[168,512]{1,0:T(8,128)S(1)}, f32[168,512]{1,0:T(8,128)S(1)}, u32[]{:S(2)}, u32[]{:S(2)}) collective-permute-start(f32[168,512]{1,0:T(8,128)S(1)} %get-tuple-element.23), channel_id=1, source_target_pairs={{0,256},{1,257},{2,258},{3,259},{4,260},{5,261},{6,262},{7,263},{8... | collective-permute-start | bytes 1032200 | tf_op jit(solution)/shard_map/ppermute | solution.py:439
  72.1 3.6 %collective-permute-start.5 = (f32[168,128]{1,0:T(8,128)S(1)}, f32[168,128]{1,0:T(8,128)S(1)}, u32[]{:S(2)}, u32[]{:S(2)}) collective-permute-start(f32[168,128]{1,0:T(8,128)S(1)} %get-tuple-element.24), channel_id=1, source_target_pairs={{0,272},{1,273},{2,274},{3,275},{4,276},{5,277},{6,278},{7,279},{8... | collective-permute-start | bytes 258056 | tf_op jit(solution)/shard_map/ppermute | solution.py:439
  75.7 3.0 %collective-permute-start.6 = (f32[24,512]{1,0:T(8,128)S(1)}, f32[24,512]{1,0:T(8,128)S(1)}, u32[]{:S(2)}, u32[]{:S(2)}) collective-permute-start(f32[24,512]{1,0:T(8,128)S(1)} %get-tuple-element.25), channel_id=1, source_target_pairs={{0,257},{1,258},{2,259},{3,260},{4,261},{5,262},{6,263},{7,264},{8... | collective-permute-start | bytes 147464 | tf_op jit(solution)/shard_map/ppermute | solution.py:439
  78.7 4.5 %collective-permute-start.7 = (f32[24,128]{1,0:T(8,128)S(1)}, f32[24,128]{1,0:T(8,128)S(1)}, u32[]{:S(2)}, u32[]{:S(2)}) collective-permute-start(f32[24,128]{1,0:T(8,128)S(1)} %get-tuple-element.26), channel_id=1, source_target_pairs={{0,273},{1,274},{2,275},{3,276},{4,277},{5,278},{6,279},{7,280},{8... | collective-permute-start | bytes 36872 | tf_op jit(solution)/shard_map/ppermute | solution.py:439
  83.2 4.8 %collective-permute-done.7.xy_ref = f32[24,128]{1,0:T(8,128)S(1)} collective-permute-done((f32[24,128]{1,0:T(8,128)S(1)}, f32[24,128]{1,0:T(8,128)S(1)}, u32[]{:S(2)}, u32[]{:S(2)}) %collective-permute-start.7) | collective-permute-done | bytes 12320 | tf_op jit(solution)/shard_map/ppermute | solution.py:439
  88.0 0.0 collective-permute-done.6.y_ref
  88.0 0.0 collective-permute-done.5.x_ref
  88.0 0.0 collective-permute-done.4.own_ref
  88.0 8.5 %all-to-all-done.1 = f32[256,1,384]{2,1,0:T(1,128)S(1)} async-done(((f32[256,1,384]{2,1,0:T(1,128)}), f32[256,1,384]{2,1,0:T(1,128)S(1)}, u32[]{:S(2)}, u32[]{:S(2)}) %all-to-all-start.1) | async-done | bytes 393248 | tf_op jit(solution)/shard_map/all_to_all | solution.py:444
  96.5 1.3 %copy-done.1 = bf16[512,1280]{1,0:T(8,128)(2,1)S(1)} copy-done((bf16[512,1280]{1,0:T(8,128)(2,1)S(1)}, bf16[512,1280]{1,0:T(8,128)(2,1)}, u32[]{:S(2)}) %copy-start.1) | copy-done | bytes 1310744
  97.8 0.0 copy-start.3
  97.8 1.0 copy-done.3
  98.8 0.0 copy-start.6
  98.8 0.9 copy-done.6
  99.7 2.0 %assemble.1 = f32[144,384]{1,0:T(8,128)} custom-call(f32[768,128]{1,0:T(8,128)S(1)} %bitcast.15, bf16[512,1280]{1,0:T(8,128)(2,1)S(1)} %copy-done.1, f32[168,512]{1,0:T(8,128)S(1)} %collective-permute-done.4.own_ref, f32[168,128]{1,0:T(8,128)S(1)} %collective-permute-done.5.x_ref, f32[24,512]{1,0:T(8,128)S(1)} %collective-permute-done.6.y_ref, ...), custom_call_target="tpu_custom_call" | custom-call | tf_op jit(solution)/shard_map/assemble/pallas_call | solution.py:422
  (1 shorter events, 0.0 us)
Async XLA Ops:
  0.0 26.5 %copy-start.4 = (f32[120,192]{1,0:T(8,128)S(1)}, f32[120,192]{1,0:T(8,128)}, u32[]{:S(2)}) copy-start(f32[120,192]{1,0:T(8,128)} %constant.19.clone.table_ref) | copy-start | bytes 276484
  0.0 29.0 %copy-start.8 = (s32[2,1,512]{2,1,0:T(1,128)S(1)}, s32[2,1,512]{2,1,0:T(1,128)}, u32[]{:S(2)}) copy-start(s32[2,1,512]{2,1,0:T(1,128)} %list_ref.3) | copy-start | bytes 12292
  0.0 26.5 %copy-start.2 = (f32[1,3,49,512]{3,0,2,1:T(1,128)S(1)}, f32[1,3,49,512]{3,0,2,1:T(1,128)}, u32[]{:S(2)}) copy-start(f32[1,3,49,512]{3,0,2,1:T(1,128)} %param.9) | copy-start | bytes 903172
  0.0 26.5 %copy-start.10 = (s32[1,256,1]{1,2,0:T(1,128)S(1)}, s32[1,256,1]{1,2,0:T(1,128)}, u32[]{:S(2)}) copy-start(s32[1,256,1]{1,2,0:T(1,128)} %param.12) | copy-start | bytes 3076
  0.0 26.5 %copy-start.9 = (s32[1,256]{1,0:T(1,128)S(1)}, s32[1,256]{1,0:T(1,128)}, u32[]{:S(2)}) copy-start(s32[1,256]{1,0:T(1,128)} %slave_ref.1) | copy-start | bytes 3076
  0.0 26.5 %copy-start.7 = (f32[1,2,36,256]{3,1,2,0:T(2,128)S(1)}, f32[1,2,36,256]{3,1,2,0:T(2,128)}, u32[]{:S(2)}) copy-start(f32[1,2,36,256]{3,1,2,0:T(2,128)} %param.10) | copy-start | bytes 221188
  2.7 53.2 %all-to-all-start = ((f32[256,1,384]{2,1,0:T(1,128)}), f32[256,1,384]{2,1,0:T(1,128)S(1)}, u32[]{:S(2)}, u32[]{:S(2)}) async-start(f32[256,1,384]{2,1,0:T(1,128)} %bitcast.3), calls=%async_computation | async-start | bytes 786432 | tf_op jit(solution)/shard_map/all_to_all | solution.py:444
  27.1 18.9 %collective-permute-start = (f32[208,256]{1,0:T(8,128)S(1)}, f32[208,256]{1,0:T(8,128)S(1)}, u32[]{:S(2)}, u32[]{:S(2)}) collective-permute-start(f32[208,256]{1,0:T(8,128)S(1)} %slave.1), channel_id=1, source_target_pairs={{0,256},{1,257},{2,258},{3,259},{4,260},{5,261},{6,262},{7,263},{8... | collective-permute-start | bytes 638984 | tf_op jit(solution)/shard_map/ppermute | solution.py:439
  29.0 13.9 %collective-permute-start.2 = (s32[2,1,512]{2,1,0:T(1,128)S(1)}, s32[2,1,512]{2,1,0:T(1,128)S(1)}, u32[]{:S(2)}, u32[]{:S(2)}) collective-permute-start(s32[2,1,512]{2,1,0:T(1,128)S(1)} %copy-done.8), channel_id=1, source_target_pairs={{0,1},{1,2},{2,3},{3,4},{4,5},{5,6},{6,7},{7,8},{8,9},{9,10},{10,1... | collective-permute-start | bytes 12296 | tf_op jit(solution)/shard_map/ppermute | solution.py:439
  32.4 10.5 %collective-permute-start.1 = (s32[2,1,512]{2,1,0:T(1,128)S(1)}, s32[2,1,512]{2,1,0:T(1,128)S(1)}, u32[]{:S(2)}, u32[]{:S(2)}) collective-permute-start(s32[2,1,512]{2,1,0:T(1,128)S(1)} %copy-done.8), channel_id=1, source_target_pairs={{0,16},{1,17},{2,18},{3,19},{4,20},{5,21},{6,22},{7,23},{8,24},{9,... | collective-permute-start | bytes 12296 | tf_op jit(solution)/shard_map/ppermute | solution.py:439
  35.9 9.9 %collective-permute-start.3 = (s32[2,1,512]{2,1,0:T(1,128)S(1)}, s32[2,1,512]{2,1,0:T(1,128)S(1)}, u32[]{:S(2)}, u32[]{:S(2)}) collective-permute-start(s32[2,1,512]{2,1,0:T(1,128)S(1)} %copy-done.8), channel_id=1, source_target_pairs={{0,17},{1,18},{2,19},{3,20},{4,21},{5,22},{6,23},{7,24},{8,25},{9,... | collective-permute-start | bytes 12296 | tf_op jit(solution)/shard_map/ppermute | solution.py:439
  58.6 37.9 %all-to-all-start.1 = ((f32[256,1,384]{2,1,0:T(1,128)}), f32[256,1,384]{2,1,0:T(1,128)S(1)}, u32[]{:S(2)}, u32[]{:S(2)}) async-start(f32[256,1,384]{2,1,0:T(1,128)} %bitcast.9), calls=%async_computation.1 | async-start | bytes 786432 | tf_op jit(solution)/shard_map/all_to_all | solution.py:444
  67.4 0.9 copy-start.5
  69.1 1.1 %copy-start = (bf16[512,1280]{1,0:T(8,128)(2,1)}, bf16[512,1280]{1,0:T(8,128)(2,1)S(1)}, u32[]{:S(2)}) copy-start(bf16[512,1280]{1,0:T(8,128)(2,1)S(1)} %get-tuple-element.22.hot_ref) | copy-start | bytes 3932164
  70.2 17.8 %collective-permute-start.4 = (f32[168,512]{1,0:T(8,128)S(1)}, f32[168,512]{1,0:T(8,128)S(1)}, u32[]{:S(2)}, u32[]{:S(2)}) collective-permute-start(f32[168,512]{1,0:T(8,128)S(1)} %get-tuple-element.23), channel_id=1, source_target_pairs={{0,256},{1,257},{2,258},{3,259},{4,260},{5,261},{6,262},{7,263},{8... | collective-permute-start | bytes 1032200 | tf_op jit(solution)/shard_map/ppermute | solution.py:439
  72.1 15.9 %collective-permute-start.5 = (f32[168,128]{1,0:T(8,128)S(1)}, f32[168,128]{1,0:T(8,128)S(1)}, u32[]{:S(2)}, u32[]{:S(2)}) collective-permute-start(f32[168,128]{1,0:T(8,128)S(1)} %get-tuple-element.24), channel_id=1, source_target_pairs={{0,272},{1,273},{2,274},{3,275},{4,276},{5,277},{6,278},{7,279},{8... | collective-permute-start | bytes 258056 | tf_op jit(solution)/shard_map/ppermute | solution.py:439
  75.7 12.3 %collective-permute-start.6 = (f32[24,512]{1,0:T(8,128)S(1)}, f32[24,512]{1,0:T(8,128)S(1)}, u32[]{:S(2)}, u32[]{:S(2)}) collective-permute-start(f32[24,512]{1,0:T(8,128)S(1)} %get-tuple-element.25), channel_id=1, source_target_pairs={{0,257},{1,258},{2,259},{3,260},{4,261},{5,262},{6,263},{7,264},{8... | collective-permute-start | bytes 147464 | tf_op jit(solution)/shard_map/ppermute | solution.py:439
  78.7 9.3 %collective-permute-start.7 = (f32[24,128]{1,0:T(8,128)S(1)}, f32[24,128]{1,0:T(8,128)S(1)}, u32[]{:S(2)}, u32[]{:S(2)}) collective-permute-start(f32[24,128]{1,0:T(8,128)S(1)} %get-tuple-element.26), channel_id=1, source_target_pairs={{0,273},{1,274},{2,275},{3,276},{4,277},{5,278},{6,279},{7,280},{8... | collective-permute-start | bytes 36872 | tf_op jit(solution)/shard_map/ppermute | solution.py:439
  96.5 1.3 %copy-start.1 = (bf16[512,1280]{1,0:T(8,128)(2,1)S(1)}, bf16[512,1280]{1,0:T(8,128)(2,1)}, u32[]{:S(2)}) copy-start(bf16[512,1280]{1,0:T(8,128)(2,1)} %copy-done) | copy-start | bytes 3932164
  97.8 1.0 copy-start.3
  98.8 0.9 copy-start.6
